TPU v7x, 32 devices: a whole 2x2x4 slice. The times are simulated.
32 devices in a mesh: group: 2 (over core), dp: 16 (over z, y, x).
Axes of the slice: x: 2, y: 2, z: 4, core: 2. Of those that a mesh axis runs over, the one named last changes fastest.
Arguments:
- patches: bfloat16 [2, 16, 512, 768], P(None, 'dp'), may hold values from -6 to 6
- segments: int32 [2, 16, 512], P(None, 'dp'), may hold values from 0 to 4, never falling along the last dimension, each value on 1 to 196 neighbouring positions
- positions: int32 [2, 16, 320], P(None, 'dp'), may hold values from 0 to 511, as said below
- owners: int32 [10752], replicated, may hold values from 0 to 10751, each once
- master: float32 [10752, 768], P(('group', 'dp')), may hold values from -0.21875 to 0.21875
- moment_one: float32 [10752, 768], P(('group', 'dp')), may hold values from -2.3841858e-06 to 2.3841858e-06
- moment_two: float32 [10752, 768], P(('group', 'dp')), may hold values from 3.8e-15 to 1.5e-14
- teacher: float32 [10752, 768], P(('group', 'dp')), may hold values from -0.21875 to 0.21875
- gains: float32 [4, 768], replicated, may hold values from 0.5 to 1.5
- gain_one: float32 [4, 768], replicated, may hold values from -2.2888184e-05 to 2.2888184e-05
- gain_two: float32 [4, 768], replicated, may hold values from 7.7e-13 to 3.1e-12
- teacher_gains: float32 [4, 768], replicated, may hold values from 0.5 to 1.5
- step_count: int32 [1], replicated, may hold values from 2 to 20
Outputs:
- loss_out: float32 [1], replicated
- clip_norm: float32 [1], replicated
- moment_one_new: float32 [10752, 768], P(('group', 'dp'))
- moment_two_new: float32 [10752, 768], P(('group', 'dp'))
- master_new: float32 [10752, 768], P(('group', 'dp'))
- teacher_new: float32 [10752, 768], P(('group', 'dp'))
- gain_one_new: float32 [4, 768], replicated
- gain_two_new: float32 [4, 768], replicated
Inputs may be any that keep to these rules, and one draw needn't show every extreme that they name: Within one row the 320 positions are distinct slots. `segments`: along a row segment ids never fall; id 4 is the padding at the row's end; each id covers 1 to 196 slots and some id covers exactly 196. owners is a permutation.
All inputs are finite; a program needn't handle non-finite values.
Results may differ from a plain program's by a relative error of at most 0.008.
The roundings to bfloat16 on the way count: a program that leaves them out, or rounds other values in their place, can miss the bound.
Values may be sent and summed in bfloat16 or wider, within the bound.
A program may use at most 320 MiB of HBM per device.

v0:
```python
import jax
import jax.numpy as jnp
from jax import lax
from jax.sharding import PartitionSpec as P

HEADS = 12
HEAD_DIM = 64
IMGS = 4
MASKED = 320
MICRO_BATCHES = 2


HIGH = lax.Precision.HIGHEST
SOFTMAX_TEMPER = 0.05
CLIP = 0.004
RATE = 0.05
BETA_ONE = 0.9
BETA_TWO = 0.999
ADAM_EPS = 1e-08
DECAY = 0.05
EMA_KEEP = 0.9
MASK_FILL = -1000000000.0


def shifted(block, axis, distance):
    devices = range(lax.axis_size(axis))
    route = [(i - distance, i) for i in devices if i - distance in devices]
    return lax.ppermute(block, axis, route)


def dense(first_op, second_op):
    return jnp.dot(first_op, second_op, preferred_element_type=jnp.float32)


def dense_left(first_op, second_op):
    return lax.dot_general(
        first_op, second_op, (((0,), (0,)), ((), ())), preferred_element_type=jnp.float32
    )


def right_dense_product(first_op, second_op):
    return lax.dot_general(
        first_op, second_op, (((1,), (1,)), ((), ())), preferred_element_type=jnp.float32
    )


def layer_stats(tensor):
    centre = tensor - jnp.mean(tensor, axis=-1, keepdims=True)
    scaled = lax.rsqrt(jnp.mean(centre * centre, axis=-1, keepdims=True) + 1e-06)
    return (centre * scaled, scaled)


def norm_back(grad_out, normed, scaled, gain_vec):
    grad_hat = grad_out * gain_vec
    inner = jnp.mean(grad_hat * normed, axis=-1, keepdims=True)
    grad_in = scaled * (grad_hat - jnp.mean(grad_hat, axis=-1, keepdims=True) - normed * inner)
    return (grad_in, jnp.sum(grad_out * normed, axis=0))


def normalize_unit(rows_in):
    length = lax.rsqrt(jnp.sum(rows_in * rows_in, axis=-1, keepdims=True) + 1e-06)
    return (rows_in * length, length)


def unpack(flat_rows):
    width = flat_rows.shape[1]
    inner_width = (flat_rows.shape[0] - 6 * width) // 2
    return (
        flat_rows[0:width],
        flat_rows[width : 2 * width],
        flat_rows[2 * width : 3 * width],
        flat_rows[3 * width : 6 * width].reshape(width, 3 * width),
        flat_rows[6 * width : 6 * width + inner_width].reshape(width, inner_width),
        flat_rows[6 * width + inner_width :],
    )


def scores_of(triple, segment_index):
    raw_scores = jnp.einsum(
        "qhd,khd->hqk", triple[:, 0], triple[:, 1], preferred_element_type=jnp.float32
    ) * HEAD_DIM ** (-0.5)
    return jnp.where(
        (segment_index[:, None] == segment_index[None, :])[None], raw_scores, MASK_FILL
    )


def forward(weights, gain_set, patch_row, segment_index, masked_slot, student):
    proj_embed, proj_out, proj_head, proj_qkv, proj_up, proj_down = weights
    slot_count = patch_row.shape[0]
    embedded = dense(patch_row, proj_embed)
    embedded = jnp.where(masked_slot[:, None] & student, gain_set[3][None, :], embedded)
    normed_one, scaled_one = layer_stats(embedded)
    attn_in = (normed_one * gain_set[0]).astype(jnp.bfloat16)
    triple = dense(attn_in, proj_qkv).astype(jnp.bfloat16).reshape(slot_count, 3, HEADS, HEAD_DIM)
    scores = scores_of(triple, segment_index)
    log_total = jax.nn.logsumexp(scores, axis=-1, keepdims=True)
    probs = jnp.exp(scores - log_total).astype(jnp.bfloat16)
    mixed_heads = jnp.einsum(
        "hqk,khd->qhd", probs, triple[:, 2], preferred_element_type=jnp.float32
    )
    mixed_heads = mixed_heads.reshape(slot_count, -1).astype(jnp.bfloat16)
    middle = embedded + dense(mixed_heads, proj_out)
    normed_two, scaled_two = layer_stats(middle)
    ffn_in = (normed_two * gain_set[1]).astype(jnp.bfloat16)
    hidden = dense(ffn_in, proj_up)
    active = jax.nn.gelu(hidden, approximate=True).astype(jnp.bfloat16)
    block_out = middle + dense(active, proj_down)
    normed_three, scaled_three = layer_stats(block_out)
    return (
        normed_one,
        scaled_one,
        attn_in,
        triple,
        log_total,
        mixed_heads,
        normed_two,
        scaled_two,
        ffn_in,
        hidden,
        active,
        normed_three,
        scaled_three,
    )


def attend_back(triple, log_total, segment_index, grad_mixed):
    slot_count = triple.shape[0]
    probs = jnp.exp(scores_of(triple, segment_index) - log_total)
    grad_heads = grad_mixed.reshape(slot_count, HEADS, HEAD_DIM)
    grad_probs = jnp.einsum(
        "qhd,khd->hqk", grad_heads, triple[:, 2], preferred_element_type=jnp.float32
    )
    grad_value = jnp.einsum(
        "hqk,qhd->khd", probs.astype(jnp.bfloat16), grad_heads, preferred_element_type=jnp.float32
    )
    grad_scores = (
        probs * (grad_probs - jnp.sum(probs * grad_probs, axis=-1, keepdims=True))
    ).astype(jnp.bfloat16)
    grad_query = jnp.einsum(
        "hqk,khd->qhd", grad_scores, triple[:, 1], preferred_element_type=jnp.float32
    ) * HEAD_DIM ** (-0.5)
    grad_key = jnp.einsum(
        "hqk,qhd->khd", grad_scores, triple[:, 0], preferred_element_type=jnp.float32
    ) * HEAD_DIM ** (-0.5)
    return (
        jnp.stack([grad_query, grad_key, grad_value], axis=1)
        .reshape(slot_count, -1)
        .astype(jnp.bfloat16)
    )


def learn_row(
    weights,
    gain_set,
    patch_row,
    segment_index,
    places,
    masked_slot,
    saved,
    sent_rows,
    memory_bank_rows,
    label_base,
    listed_count,
):
    proj_embed, proj_out, proj_head, proj_qkv, proj_up, proj_down = weights
    (
        normed_one,
        scaled_one,
        attn_in,
        triple,
        log_total,
        mixed_heads,
        normed_two,
        scaled_two,
        ffn_in,
        hidden,
        active,
        normed_three,
        scaled_three,
    ) = saved
    width = patch_row.shape[1]
    head_in = (normed_three * gain_set[2]).astype(jnp.bfloat16)
    prediction_head = dense(head_in, proj_head)
    valid_mask = (segment_index[places] < IMGS).astype(jnp.float32)
    differ = prediction_head[places] - sent_rows.astype(jnp.float32)
    magnitude = jnp.abs(differ)
    huber_term = jnp.where(magnitude < 1.0, 0.5 * differ * differ, magnitude - 0.5)
    regress = jnp.sum(valid_mask[:, None] * huber_term)
    grad_pred = (
        jnp.zeros_like(prediction_head)
        .at[places]
        .add(valid_mask[:, None] * jnp.clip(differ, -1.0, 1.0) / (listed_count * width))
    )
    member = (segment_index[None, :] == jnp.arange(IMGS, dtype=jnp.int32)[:, None]).astype(
        jnp.float32
    )
    sizes = jnp.sum(member, axis=1, keepdims=True)
    normalized_prediction, length = normalize_unit(
        jnp.dot(member, prediction_head, precision=HIGH) / sizes
    )
    class_logits = (
        right_dense_product(normalized_prediction.astype(jnp.bfloat16), memory_bank_rows)
        / SOFTMAX_TEMPER
    )
    selected_slots = (
        jnp.arange(memory_bank_rows.shape[0], dtype=jnp.int32)[None, :]
        == (label_base + jnp.arange(IMGS, dtype=jnp.int32))[:, None]
    ).astype(jnp.float32)
    contrast = jnp.sum(
        jax.nn.logsumexp(class_logits, axis=-1) - jnp.sum(class_logits * selected_slots, axis=1)
    )
    grad_logits = (
        (jax.nn.softmax(class_logits, axis=-1) - selected_slots)
        / (memory_bank_rows.shape[0] * MICRO_BATCHES)
        / SOFTMAX_TEMPER
    ).astype(jnp.bfloat16)
    grad_unit = dense(grad_logits, memory_bank_rows)
    grad_pooled = length * (
        grad_unit
        - normalized_prediction * jnp.sum(grad_unit * normalized_prediction, axis=1, keepdims=True)
    )
    grad_pred = grad_pred + jnp.dot(member.T, grad_pooled / sizes, precision=HIGH)
    grad_low = grad_pred.astype(jnp.bfloat16)
    grad_head = dense_left(head_in, grad_low)
    grad_top, gain_three = norm_back(
        right_dense_product(grad_low, proj_head), normed_three, scaled_three, gain_set[2]
    )
    grad_down_out = grad_top.astype(jnp.bfloat16)
    grad_down = dense_left(active, grad_down_out)
    gelu_value, gelu_pull = jax.vjp(lambda inner: jax.nn.gelu(inner, approximate=True), hidden)
    grad_hidden = gelu_pull(right_dense_product(grad_down_out, proj_down))[0].astype(jnp.bfloat16)
    grad_up = dense_left(ffn_in, grad_hidden)
    grad_ffn_norm, gain_two = norm_back(
        right_dense_product(grad_hidden, proj_up), normed_two, scaled_two, gain_set[1]
    )
    grad_middle = grad_top + grad_ffn_norm
    grad_out_low = grad_middle.astype(jnp.bfloat16)
    grad_out = dense_left(mixed_heads, grad_out_low)
    grad_mixed = right_dense_product(grad_out_low, proj_out).astype(jnp.bfloat16)
    grad_triple = attend_back(triple, log_total, segment_index, grad_mixed)
    grad_qkv = dense_left(attn_in, grad_triple)
    grad_attn_norm, gain_one = norm_back(
        right_dense_product(grad_triple, proj_qkv), normed_one, scaled_one, gain_set[0]
    )
    grad_start = grad_middle + grad_attn_norm
    grad_token = jnp.sum(jnp.where(masked_slot[:, None], grad_start, 0.0), axis=0)
    grad_embed_out = jnp.where(masked_slot[:, None], 0.0, grad_start).astype(jnp.bfloat16)
    grad_embed = dense_left(patch_row, grad_embed_out)
    grad_rows = jnp.concatenate(
        [
            grad_embed,
            grad_out,
            grad_head,
            grad_qkv.reshape(-1, width),
            grad_up.reshape(-1, width),
            grad_down,
        ],
        axis=0,
    )
    return (grad_rows, jnp.stack([gain_one, gain_two, gain_three, grad_token]), regress, contrast)


def bank_of(target, segment_index):
    member = (segment_index[None, :] == jnp.arange(IMGS, dtype=jnp.int32)[:, None]).astype(
        jnp.float32
    )
    pooled_target = jnp.dot(member, target.astype(jnp.float32), precision=HIGH) / jnp.sum(
        member, axis=1, keepdims=True
    )
    return normalize_unit(pooled_target)[0].astype(jnp.bfloat16)


def slot_flags(places, slot_count):
    return jnp.any(places[:, None] == jnp.arange(slot_count, dtype=jnp.int32)[None, :], axis=0)


def adam_update(weight, first_state, second_state, gradient, step_value, decay_rate):
    first_state = BETA_ONE * first_state + (1.0 - BETA_ONE) * gradient
    second_state = BETA_TWO * second_state + (1.0 - BETA_TWO) * gradient * gradient
    fix_one = 1.0 - jnp.power(BETA_ONE, step_value)
    fix_two = 1.0 - jnp.power(BETA_TWO, step_value)
    update = first_state / fix_one / (jnp.sqrt(second_state / fix_two) + ADAM_EPS)
    return (weight - RATE * (update + decay_rate * weight), first_state, second_state)


def body(
    patches,
    segments,
    positions,
    owners,
    master,
    moment_one,
    moment_two,
    teacher,
    gains,
    gain_one,
    gain_two,
    teacher_gains,
    step_count,
):
    core = lax.axis_index("group")
    is_student = core == 1
    master_all, teacher_all = (
        lax.all_gather(master.astype(jnp.bfloat16), ("group", "dp"), axis=0, tiled=True),
        lax.all_gather(teacher.astype(jnp.bfloat16), ("group", "dp"), axis=0, tiled=True),
    )
    row_total = owners.shape[0]
    inverse = (
        jnp.zeros((row_total,), jnp.int32).at[owners].set(jnp.arange(row_total, dtype=jnp.int32))
    )
    width = patches.shape[3]
    slot_count = patches.shape[2]
    device_count = lax.axis_size("group") * lax.axis_size("dp")
    own_rows = row_total // device_count
    listed_count = jnp.float32(MASKED * lax.axis_size("dp") * MICRO_BATCHES)
    label_base = lax.axis_index("dp") * IMGS
    weights = unpack(jnp.where(is_student, master_all, teacher_all)[inverse])
    gain_set = jnp.where(is_student, gains, teacher_gains)
    grad_total = jnp.zeros((row_total, width), jnp.float32)
    gain_grad = jnp.zeros((4, width), jnp.float32)
    loss_local = jnp.zeros((), jnp.float32)
    for batch_idx in range(MICRO_BATCHES):
        patch_row = patches[batch_idx, 0]
        segment_index = segments[batch_idx, 0]
        places = positions[batch_idx, 0]
        masked_slot = slot_flags(places, slot_count)
        saved = forward(weights, gain_set, patch_row, segment_index, masked_slot, is_student)
        target = saved[11].astype(jnp.bfloat16)
        bank_own = bank_of(target, segment_index)
        sent_rows, sent_bank = shifted((target[places], bank_own), "group", 1)
        memory_bank_rows = lax.all_gather(sent_bank, "dp", axis=0, tiled=True)

        def learn_branch():
            return learn_row(
                weights,
                gain_set,
                patch_row,
                segment_index,
                places,
                masked_slot,
                saved,
                sent_rows,
                memory_bank_rows,
                label_base,
                listed_count,
            )

        def skip_branch():
            return (
                jnp.zeros((row_total, width), jnp.float32),
                jnp.zeros((4, width), jnp.float32),
                jnp.zeros((), jnp.float32),
                jnp.zeros((), jnp.float32),
            )

        grad_rows, grad_gains_part, regress, contrast = lax.cond(
            is_student, learn_branch, skip_branch
        )
        grad_total = grad_total + grad_rows
        gain_grad = gain_grad + grad_gains_part
        loss_local = (
            loss_local
            + regress / (listed_count * width)
            + contrast / (memory_bank_rows.shape[0] * MICRO_BATCHES)
        )
    blocked = grad_total[owners].reshape(device_count, own_rows, width)
    owned_grad = lax.psum_scatter(
        blocked, ("group", "dp"), scatter_dimension=0, tiled=True
    ).reshape(own_rows, width)
    square_own = jnp.sum(owned_grad * owned_grad)
    gain_sum, loss_sum = lax.psum((gain_grad, loss_local), ("group", "dp"))
    square_sum = lax.psum(square_own, ("group", "dp"))
    grad_norm = jnp.sqrt(square_sum + jnp.sum(gain_sum * gain_sum))
    factor = jnp.minimum(1.0, CLIP / grad_norm)
    step_value = step_count[0].astype(jnp.float32)
    master_new, one_new, two_new = adam_update(
        master, moment_one, moment_two, owned_grad * factor, step_value, DECAY
    )
    gone_new, gtwo_new = adam_update(gains, gain_one, gain_two, gain_sum * factor, step_value, 0.0)[
        1:
    ]
    teacher_new = EMA_KEEP * teacher + (1.0 - EMA_KEEP) * master_new
    return (
        loss_sum.reshape(1),
        grad_norm.reshape(1),
        one_new,
        two_new,
        master_new,
        teacher_new,
        gone_new,
        gtwo_new,
    )


def solution(mesh):
    in_specs = (
        P(None, "dp", None, None),
        P(None, "dp", None),
        P(None, "dp", None),
        P(),
        P(("group", "dp"), None),
        P(("group", "dp"), None),
        P(("group", "dp"), None),
        P(("group", "dp"), None),
        P(),
        P(),
        P(),
        P(),
        P(),
    )
    out_specs = (
        P(),
        P(),
        P(("group", "dp"), None),
        P(("group", "dp"), None),
        P(("group", "dp"), None),
        P(("group", "dp"), None),
        P(),
        P(),
    )
    return jax.shard_map(body, mesh=mesh, in_specs=in_specs, out_specs=out_specs, check_vma=False)
```

profile of v0, /device:TPU:0, one launch (start us, length us, event | category | flops | bytes accessed | tf_op | source)
XLA Modules:
  0.0 1424.0 jit_solution(17538444863459090412)
XLA Ops:
  10.5 39.8 %scatter_custom_fusion.2 = s32[10752]{0:T(1024)S(1)} fusion(s32[10752]{0:T(1024)S(1)} %compare_select_fusion.3, s32[10752]{0:T(1024)S(1)} %iota.51, s32[]{:T(128)} %constant.272.clone.1), kind=kCustom, calls=%fused_computation.391 | custom fusion | bytes 43012 | tf_op jit(solution)/shard_map/scatter | solution.py:309
  58.4 69.2 %all-gather.5.cloned.1.call-done = bf16[10752,768]{1,0:T(8,128)(2,1)} async-done(((bf16[336,768]{1,0:T(8,128)(2,1)}), bf16[10752,768]{1,0:T(8,128)(2,1)}) %all-gather.5.cloned.1.call-update) | async-done | bytes 16515088 | tf_op jit(solution)/shard_map/all_gather | solution.py:304
  127.6 115.1 %all-gather.7.cloned.1.call-done = bf16[10752,768]{1,0:T(8,128)(2,1)} async-done(((bf16[336,768]{1,0:T(8,128)(2,1)}), bf16[10752,768]{1,0:T(8,128)(2,1)}) %all-gather.7.cloned.1.call-update) | async-done | bytes 16515088 | tf_op jit(solution)/shard_map/all_gather | solution.py:305
  242.7 14.0 broadcast_select_fusion
  256.8 47.0 %gather_fusion.4 = bf16[10752,768]{1,0:T(8,128)(2,1)} fusion(bf16[10752,768]{1,0:T(8,128)(2,1)} %broadcast_select_fusion, s32[11264]{0:T(1024)S(1)} %pad_clamp_fusion.3), kind=kCustom, calls=%fused_computation.4 | custom fusion | bytes 33073152 | tf_op jit(solution)/shard_map/gather | solution.py:317
  303.7 8.0 fusion.216
  344.2 7.3 exponential_reduce_fusion.3
  351.6 7.9 fusion.183
  368.8 6.2 fusion.159
  375.0 7.3 exponential_reduce_fusion.2
  382.4 7.9 fusion.182
  392.9 8.5 reshape.540
  405.4 9.0 fusion.167
  425.2 9.4 fusion.175
  449.0 40.7 %all-gather = bf16[16,4,768]{2,1,0:T(4,128)(2,1)} all-gather(bf16[1,4,768]{2,1,0:T(4,128)(2,1)S(1)} %bitcast.299), channel_id=1, replica_groups=mesh['group'=2,'dp'=16] {'dp'}, dimensions={0}, use_global_device_ids=true | all-gather | bytes 104448 | tf_op jit(solution)/shard_map/all_gather | solution.py:331
  489.7 38.3 %all-gather.1 = bf16[16,4,768]{2,1,0:T(4,128)(2,1)} all-gather(bf16[1,4,768]{2,1,0:T(4,128)(2,1)S(1)} %bitcast.300), channel_id=1, replica_groups=mesh['group'=2,'dp'=16] {'dp'}, dimensions={0}, use_global_device_ids=true | all-gather | bytes 104448 | tf_op jit(solution)/shard_map/all_gather | solution.py:331
  529.2 25.3 %conditional.2 = (f32[4,768]{1,0:T(4,128)S(1)}, f32[]{:T(128)}, f32[]{:T(128)}, f32[10752,768]{1,0:T(8,128)}) conditional(s32[]{:T(128)} %convert_element_type.252, () %tuple.34, (pred[512]{0:T(512)(128)(4,1)}, f32[512]{0:T(512)}, f32[512,1]{0,1:T(1,128)}, f32[512,1]{0,1:T(1,128)}, s32[1,1,512]{2,1,0:T(1,128)S(1)}, ...), branch_computations={%region_12.13_spmd, %region_13.35_spmd} | conditional | flops 19070142464 | bytes 605004032 | solution.py:356
  529.2 10.8 broadcast.594.clone
  555.1 14.4 %conditional.3 = (f32[4,768]{1,0:T(4,128)S(1)}, f32[]{:T(128)}, f32[]{:T(128)}, f32[10752,768]{1,0:T(8,128)}) conditional(s32[]{:T(128)} %convert_element_type.252, () %tuple.36, (pred[512]{0:T(512)(128)(4,1)}, f32[512]{0:T(512)}, f32[512,1]{0,1:T(1,128)}, f32[512,1]{0,1:T(1,128)}, s32[1,1,512]{2,1,0:T(1,128)S(1)}, ...), branch_computations={%region_46.47_spmd, %region_47.69_spmd} | conditional | flops 19070142464 | bytes 613257856 | solution.py:356
  555.1 10.9 broadcast.614.clone
  569.5 33.0 %add.370 = f32[10752,768]{1,0:T(8,128)} add(f32[10752,768]{1,0:T(8,128)} %get-tuple-element.766, f32[10752,768]{1,0:T(8,128)} %get-tuple-element.768) | non-fusion elementwise | flops 8257536 | bytes 99090432 | tf_op jit(solution)/shard_map/add | solution.py:359
  602.5 49.4 %gather_fusion.7 = f32[10752,768]{1,0:T(8,128)} fusion(f32[10752,768]{1,0:T(8,128)} %add.370, s32[11264]{0:T(1024)S(1)} %copy-done.71), kind=kCustom, calls=%fused_computation.7 | custom fusion | bytes 66103296 | tf_op jit(solution)/shard_map/gather | solution.py:366
  652.9 713.5 %reduce-scatter.2.cloned.1.call-done = f32[1,336,768]{2,1,0:T(8,128)} async-done(((f32[32,336,768]{2,1,0:T(8,128)}), f32[1,336,768]{2,1,0:T(8,128)}) %reduce-scatter.2.cloned.1.call-update) | async-done | bytes 1032208 | tf_op jit(solution)/shard_map/reduce_scatter | solution.py:367
  1368.5 40.6 %all-reduce = (f32[1]{0:T(128)}, f32[]{:T(128)}, f32[4,768]{1,0:T(4,128)S(1)}) all-reduce(f32[1]{0:T(128)} %bitcast.76, f32[]{:T(128)} %multiply_reduce_fusion.30, f32[4,768]{1,0:T(4,128)S(1)} %add.371), channel_id=1, replica_groups=mesh['group'=2,'dp'=16] {'group','dp'}, use_global_device_ids=true, to_apply=%region_69.70 | all-reduce | flops 3074 | bytes 24592 | tf_op jit(solution)/shard_map/psum | solution.py:371
  (244 shorter events, 93.4 us)
Async XLA Ops:
  7.2 43.2 %copy-start.99 = (s32[2,1,320]{2,1,0:T(1,128)S(1)}, s32[2,1,320]{2,1,0:T(1,128)}, u32[]{:S(2)}) copy-start(s32[2,1,320]{2,1,0:T(1,128)} %param.19) | copy-start | bytes 7684
  7.2 44.4 %copy-start.110 = (s32[2,1,512]{2,1,0:T(1,128)S(1)}, s32[2,1,512]{2,1,0:T(1,128)}, u32[]{:S(2)}) copy-start(s32[2,1,512]{2,1,0:T(1,128)} %param.18) | copy-start | bytes 12292
  7.2 45.8 %copy-start.100 = (f32[4,768]{1,0:T(4,128)S(1)}, f32[4,768]{1,0:T(4,128)}, u32[]{:S(2)}) copy-start(f32[4,768]{1,0:T(4,128)} %param.25) | copy-start | bytes 36868
  7.2 45.8 %copy-start.101 = (f32[4,768]{1,0:T(4,128)S(1)}, f32[4,768]{1,0:T(4,128)}, u32[]{:S(2)}) copy-start(f32[4,768]{1,0:T(4,128)} %param.28) | copy-start | bytes 36868
  7.2 49.9 %copy-start.58 = (bf16[2,1,512,768]{3,2,1,0:T(8,128)(2,1)S(1)}, bf16[2,1,512,768]{3,2,1,0:T(8,128)(2,1)}, u32[]{:S(2)}) copy-start(bf16[2,1,512,768]{3,2,1,0:T(8,128)(2,1)} %param.17) | copy-start | bytes 4718596
  7.2 120.4 %all-gather.5.cloned.1.call-start = ((), (), s32[]{:S(2)}) async-start(), calls=%async_computation.1 | async-start | bytes 17031168 | tf_op jit(solution)/shard_map/all_gather | solution.py:304
  9.5 233.2 %all-gather.7.cloned.1.call-start = ((), (), s32[]{:S(2)}) async-start(), calls=%async_computation.2 | async-start | bytes 17031168 | tf_op jit(solution)/shard_map/all_gather | solution.py:305
  10.4 1356.0 %reduce-scatter.2.cloned.1.call-start = ((), (), s32[]{:S(2)}) async-start(), calls=%async_computation.3 | async-start | bytes 34062336 | tf_op jit(solution)/shard_map/reduce_scatter | solution.py:367
  51.6 390.8 %copy-start = (s32[1,1,512]{2,1,0:T(1,128)}, s32[1,1,512]{2,1,0:T(1,128)S(1)}, u32[]{:S(2)}) copy-start(s32[1,1,512]{2,1,0:T(1,128)S(1)} %get-tuple-element.872) | copy-start | bytes 6148
  331.0 30.7 %copy-start.48 = (bf16[512,768]{0,1:T(8,128)(2,1)}, bf16[512,768]{0,1:T(8,128)(2,1)S(1)}, u32[]{:S(2)}) copy-start(bf16[512,768]{0,1:T(8,128)(2,1)S(1)} %get-tuple-element.822) | copy-start | bytes 2359300
  419.6 29.3 %collective-permute-start = (bf16[4,768]{1,0:T(4,128)(2,1)S(1)}, bf16[4,768]{1,0:T(4,128)(2,1)S(1)}, u32[]{:S(2)}, u32[]{:S(2)}) collective-permute-start(bf16[4,768]{1,0:T(4,128)(2,1)S(1)} %multiply_convert_fusion.25), channel_id=1, source_target_pairs={{0,16},{1,17},{2,18},{3,19},{4,20},{5,21},{6,22},{7,23},{8,24},{9,... | collective-permute-start | bytes 18440 | tf_op jit(solution)/shard_map/ppermute | solution.py:28
  423.9 104.1 %collective-permute-start.1 = (bf16[320,768]{1,0:T(8,128)(2,1)S(1)}, bf16[320,768]{1,0:T(8,128)(2,1)S(1)}, u32[]{:S(2)}, u32[]{:S(2)}) collective-permute-start(bf16[320,768]{1,0:T(8,128)(2,1)S(1)} %gather_fusion.5), channel_id=1, source_target_pairs={{0,16},{1,17},{2,18},{3,19},{4,20},{5,21},{6,22},{7,23},{8,24},{9,... | collective-permute-start | bytes 1474568 | tf_op jit(solution)/shard_map/ppermute | solution.py:28
  442.9 86.3 %copy-start.73 = (f32[4,768]{1,0:T(4,128)S(1)}, f32[4,768]{1,0:T(4,128)}, u32[]{:S(2)}) copy-start(f32[4,768]{1,0:T(4,128)} %copy-done.72) | copy-start | bytes 36868
  445.5 109.0 %collective-permute-start.3 = (bf16[320,768]{1,0:T(8,128)(2,1)}, bf16[320,768]{1,0:T(8,128)(2,1)}, u32[]{:S(2)}, u32[]{:S(2)}) collective-permute-start(bf16[320,768]{1,0:T(8,128)(2,1)} %gather_fusion.6), channel_id=1, source_target_pairs={{0,16},{1,17},{2,18},{3,19},{4,20},{5,21},{6,22},{7,23},{8,24},{9,... | collective-permute-start | bytes 1474568 | tf_op jit(solution)/shard_map/ppermute | solution.py:28
  447.7 42.1 %collective-permute-start.2 = (bf16[4,768]{1,0:T(4,128)(2,1)S(1)}, bf16[4,768]{1,0:T(4,128)(2,1)S(1)}, u32[]{:S(2)}, u32[]{:S(2)}) collective-permute-start(bf16[4,768]{1,0:T(4,128)(2,1)S(1)} %multiply_convert_fusion.24), channel_id=1, source_target_pairs={{0,16},{1,17},{2,18},{3,19},{4,20},{5,21},{6,22},{7,23},{8,24},{9,... | collective-permute-start | bytes 18440 | tf_op jit(solution)/shard_map/ppermute | solution.py:28
  529.2 25.4 %copy-start.66 = (f32[12,512]{1,0:T(8,128)S(1)}, f32[12,512]{1,0:T(8,128)}, u32[]{:S(2)}) copy-start(f32[12,512]{1,0:T(8,128)} %copy-done.65) | copy-start | bytes 73732
  529.2 25.4 %copy-start.67 = (bf16[16,4,768]{2,1,0:T(4,128)(2,1)S(1)}, bf16[16,4,768]{2,1,0:T(4,128)(2,1)}, u32[]{:S(2)}) copy-start(bf16[16,4,768]{2,1,0:T(4,128)(2,1)} %all-gather.1) | copy-start | bytes 294916
  529.2 25.4 %copy-start.70 = (f32[12,512]{1,0:T(8,128)S(1)}, f32[12,512]{1,0:T(8,128)}, u32[]{:S(2)}) copy-start(f32[12,512]{1,0:T(8,128)} %copy-done.69) | copy-start | bytes 73732
  569.5 33.0 %copy-start.71 = (s32[11264]{0:T(1024)S(1)}, s32[11264]{0:T(1024)}, u32[]{:S(2)}) copy-start(s32[11264]{0:T(1024)} %pad_clamp_fusion.2) | copy-start | bytes 135172
  651.9 759.2 %copy-start.102 = (f32[4,768]{1,0:T(4,128)S(1)}, f32[4,768]{1,0:T(4,128)}, u32[]{:S(2)}) copy-start(f32[4,768]{1,0:T(4,128)} %param.27) | copy-start | bytes 36868
  651.9 759.2 %copy-start.103 = (f32[4,768]{1,0:T(4,128)S(1)}, f32[4,768]{1,0:T(4,128)}, u32[]{:S(2)}) copy-start(f32[4,768]{1,0:T(4,128)} %param.26) | copy-start | bytes 36868
  651.9 759.9 %copy-start.36 = (f32[336,768]{1,0:T(8,128)S(1)}, f32[336,768]{1,0:T(8,128)}, u32[]{:S(2)}) copy-start(f32[336,768]{1,0:T(8,128)} %param.21) | copy-start | bytes 3096580
  651.9 759.9 %copy-start.38 = (f32[336,768]{1,0:T(8,128)S(1)}, f32[336,768]{1,0:T(8,128)}, u32[]{:S(2)}) copy-start(f32[336,768]{1,0:T(8,128)} %param.24) | copy-start | bytes 3096580
  651.9 759.8 %copy-start.60 = (f32[336,768]{1,0:T(8,128)S(1)}, f32[336,768]{1,0:T(8,128)}, u32[]{:S(2)}) copy-start(f32[336,768]{1,0:T(8,128)} %param.23) | copy-start | bytes 3096580
  (56 other events, 333.7 us)
Sparse Core Ops, SparseCore 0:
  11.5 116.0 all-gather.4
  131.1 111.5 all-gather.6
  652.1 714.2 reduce-scatter.1
where the time goes:
time: 1440 us; the launch traced here: 1420 us
  waiting for transfers between devices  898 us (62%)
  local copies, waits for them, and re-layouts  201 us (14%)
  blocking collectives  120 us (8%)
  other arithmetic  92.1 us (6%)
  matrix products  69.9 us (5%)
  between operations  18.7 us (1%)
  loops' own time  17.9 us (1%)
    reduce_scatter x1, waiting for transfers between devices, body(): lax.psum_scatter(blocked, ('group', 'dp'), scatter_dimension=0, tiled=True)  714 us
    all_gather x1, waiting for transfers between devices, body(): lax.all_gather(teacher.astype(jnp.bfloat16), ('group', 'dp'), axis=0, til...  115 us
    all_gather x2, blocking collectives, body(): memory_bank_rows = lax.all_gather(sent_bank, 'dp', axis=0, tiled=True)  79 us
    all_gather x1, waiting for transfers between devices, body(): lax.all_gather(master.astype(jnp.bfloat16), ('group', 'dp'), axis=0, tile...  69.2 us
    gather x1, local copies, waits for them, and re-layouts, body(): blocked = grad_total[owners].reshape(device_count, own_rows, width)  49.4 us
    gather x1, local copies, waits for them, and re-layouts, body(): weights = unpack(jnp.where(is_student, master_all, teacher_all)[inverse])  47 us
    dot_general x10, matrix products, dense(): return jnp.dot(first_op, second_op, preferred_element_type=jnp.float32)  41.1 us
    psum x1, blocking collectives, body(): gain_sum, loss_sum = lax.psum((gain_grad, loss_local), ('group', 'dp'))  40.6 us
  transfers between devices with their start and end apart: 7, of which 3 were waited for; matrix products, arithmetic and copies ran while one was open for 6% of the time, Pallas kernels for 0%

commit v1 on v0

v1 whole, which is shorter than its diff:
```python
import functools

import jax
import jax.numpy as jnp
from jax import lax
from jax.experimental import pallas as pl
from jax.experimental.pallas import tpu as pltpu
from jax.sharding import PartitionSpec as P

HEADS = 12
HEAD_DIM = 64
IMGS = 4
MASKED = 320
MICRO_BATCHES = 2
LANES = 128
SUBLANES = 8

SOFTMAX_TEMPER = 0.05
CLIP = 0.004
RATE = 0.05
BETA_ONE = 0.9
BETA_TWO = 0.999
ADAM_EPS = 1e-08
DECAY = 0.05
EMA_KEEP = 0.9
MASK_FILL = -1000000000.0

BF = jnp.bfloat16
F32 = jnp.float32
VMEM_LIMIT = 67_000_000
GELU_A = 0.7978845608028654
GELU_B = 0.044715


def nn(a, b):
    return jnp.dot(a, b, preferred_element_type=F32)


def nt(a, b):
    return lax.dot_general(a, b, (((1,), (1,)), ((), ())), preferred_element_type=F32)


def unit_list(width, inner):
    cuts = inner // width
    return (
        [(0, 1), (width, 1), (2 * width, 1)]
        + [(3 * width + j, 3) for j in range(3)]
        + [(6 * width + j, cuts) for j in range(cuts)]
        + [(6 * width + inner + width * j, 1) for j in range(cuts)]
    )


def any_spec():
    return pl.BlockSpec(memory_space=pl.ANY)


def smem_spec():
    return pl.BlockSpec(memory_space=pltpu.SMEM)


def place_kernel(units, role, owners, teach, learn, out, rows_scr, inbuf, stage, outbuf, in_sem, out_sem):
    blocks, rows, width = teach.shape
    cols = width // LANES

    def fetch(b, slot):
        @pl.when(role[0] == 0)
        def _():
            pltpu.make_async_copy(teach.at[b], inbuf.at[slot], in_sem.at[slot]).start()

        @pl.when(role[0] != 0)
        def _():
            pltpu.make_async_copy(learn.at[b], inbuf.at[slot], in_sem.at[slot]).start()

    fetch(0, 0)

    def block(b, carry):
        slot = lax.rem(b, 2)
        pltpu.make_async_copy(teach.at[b], inbuf.at[slot], in_sem.at[slot]).wait()

        @pl.when(b + 1 < blocks)
        def _():
            fetch(b + 1, 1 - slot)

        for c in range(cols):
            stage[pl.ds(c, rows, stride=SUBLANES), :] = inbuf[slot, :, c * LANES : (c + 1) * LANES].astype(F32)

        def move(r, carry):
            dst = pl.multiple_of(owners[b * rows + r] * SUBLANES, SUBLANES)
            src = pl.multiple_of(r * SUBLANES, SUBLANES)
            rows_scr[pl.ds(dst, SUBLANES), :] = stage[pl.ds(src, SUBLANES), :]
            return carry

        return lax.fori_loop(0, rows, move, carry, unroll=14)

    lax.fori_loop(0, blocks, block, 0)
    for u, (first, step) in enumerate(units):
        slot = u % 2
        if u >= 2:
            pltpu.make_async_copy(outbuf.at[slot], out.at[u - 2], out_sem.at[slot]).wait()
        for c in range(cols):
            outbuf[slot, :, c * LANES : (c + 1) * LANES] = rows_scr[
                pl.ds(first * SUBLANES + c, width, stride=step * SUBLANES), :
            ].astype(BF)
        pltpu.make_async_copy(outbuf.at[slot], out.at[u], out_sem.at[slot]).start()
    for u in (len(units) - 2, len(units) - 1):
        pltpu.make_async_copy(outbuf.at[u % 2], out.at[u], out_sem.at[u % 2]).wait()


def place_weights(role, owners, teach, learn, units):
    blocks, rows, width = teach.shape
    total = owners.shape[0]
    return pl.pallas_call(
        functools.partial(place_kernel, units),
        name="place_weights",
        out_shape=jax.ShapeDtypeStruct((len(units), width, width), BF),
        in_specs=[smem_spec(), smem_spec(), any_spec(), any_spec()],
        out_specs=any_spec(),
        scratch_shapes=[
            pltpu.VMEM((total * SUBLANES, LANES), F32),
            pltpu.VMEM((2, rows, width), BF),
            pltpu.VMEM((rows * SUBLANES, LANES), F32),
            pltpu.VMEM((2, width, width), BF),
            pltpu.SemaphoreType.DMA((2,)),
            pltpu.SemaphoreType.DMA((2,)),
        ],
        compiler_params=pltpu.CompilerParams(vmem_limit_bytes=VMEM_LIMIT),
    )(role, owners, teach, learn)


def layer_stats(tensor):
    centre = tensor - jnp.mean(tensor, axis=-1, keepdims=True)
    scaled = lax.rsqrt(jnp.mean(centre * centre, axis=-1, keepdims=True) + 1e-06)
    return centre * scaled, scaled


def column_of(row):
    n = row.shape[1]
    eye = lax.broadcasted_iota(jnp.int32, (n, n), 0) == lax.broadcasted_iota(jnp.int32, (n, n), 1)
    return jnp.sum(jnp.where(eye, row, 0), axis=1, keepdims=True)


def flag_column(pos, slots):
    hit = lax.broadcasted_iota(jnp.int32, (slots, pos.shape[1]), 0) == pos
    return jnp.max(jnp.where(hit, 1, 0), axis=1, keepdims=True)


def fill_bias(bias, seg_col, seg_row):
    bias[...] = jnp.where(seg_col == seg_row, 0.0, MASK_FILL)


def half(x, h):
    low = lax.broadcasted_iota(jnp.int32, (1, LANES), 1) < HEAD_DIM
    keep = low if h == 0 else jnp.logical_not(low)
    return jnp.where(keep, x, jnp.zeros_like(x))


def fwd_kernel(role, patch, seg, pos, gain, w_hbm, e_out, qkv, lse, o_out, x1_out, x2_out, tgt, bank, w, bias, sem):
    i = pl.program_id(0)
    slots, width = patch.shape[1:]
    pieces = w_hbm.shape[0]
    cuts = (pieces - 6) // 2
    order = [0, 3, 4, 5, 1]
    for j in range(cuts):
        order += [6 + j, 6 + cuts + j]

    @pl.when(i == 0)
    def _():
        for u in order:
            pltpu.make_async_copy(w_hbm.at[u], w.at[u], sem.at[u]).start()

    def need(u):
        @pl.when(i == 0)
        def _():
            pltpu.make_async_copy(w_hbm.at[u], w.at[u], sem.at[u]).wait()

    seg_row = seg[0]
    seg_col = column_of(seg_row)
    fill_bias(bias, seg_col, seg_row)
    flags = flag_column(pos[0], slots) * role[0]
    need(0)
    e = nn(patch[0], w[0])
    e = jnp.where(flags > 0, gain[3:4, :], e)
    e_out[0] = e
    a = (layer_stats(e)[0] * gain[0:1, :]).astype(BF)
    for j in range(3):
        need(3 + j)
        qkv[j] = nn(a, w[3 + j]).astype(BF)

    def pair(p, carry):
        cs = pl.ds(pl.multiple_of(p * LANES, LANES), LANES)
        q2, k2, v2 = qkv[0, :, cs], qkv[1, :, cs], qkv[2, :, cs]
        k2 = k2 * jnp.asarray(HEAD_DIM**-0.5, BF)
        v_t = v2.T
        outs = []
        for h in range(2):
            s = nt(half(k2, h), q2) + bias[...]
            top = jnp.max(s, axis=0, keepdims=True)
            ex = jnp.exp(s - top)
            total = jnp.sum(ex, axis=0, keepdims=True)
            lse[0, pl.ds(2 * p + h, 1), :] = top + jnp.log(total)
            probs = (ex * (1.0 / total)).astype(BF)
            outs.append(nn(v_t[h * HEAD_DIM : (h + 1) * HEAD_DIM, :], probs))
        o_out[0, :, cs] = jnp.concatenate(outs, axis=0).T.astype(BF)
        return carry

    lax.fori_loop(0, HEADS // 2, pair, 0)
    need(1)
    x1 = e_out[0] + nn(o_out[0], w[1])
    x1_out[0] = x1
    a2 = (layer_stats(x1)[0] * gain[1:2, :]).astype(BF)
    acc = x1
    for j in range(cuts):
        need(6 + j)
        hid = nn(a2, w[6 + j])
        act = (hid * (0.5 * (1.0 + jnp.tanh(GELU_A * (hid + GELU_B * hid * hid * hid))))).astype(BF)
        need(6 + cuts + j)
        acc = acc + nn(act, w[6 + cuts + j])
    x2_out[0] = acc

    @pl.when(role[0] == 0)
    def _():
        t = layer_stats(x2_out[0])[0].astype(BF)
        tgt[0] = t
        t = t.astype(F32)
        for m in range(IMGS):
            inside = seg_col == m
            size = jnp.sum(jnp.where(inside, 1.0, 0.0), axis=0, keepdims=True)
            pooled = jnp.sum(jnp.where(inside, t, 0.0), axis=0, keepdims=True) / size
            unit = pooled * lax.rsqrt(jnp.sum(pooled * pooled, axis=-1, keepdims=True) + 1e-06)
            bank[0, m : m + 1, :] = unit.astype(BF)


def forward(role, patch, seg, pos, gain, w):
    batches, slots, width = patch.shape
    pieces = w.shape[0]
    tok = lambda dt: jax.ShapeDtypeStruct((batches, slots, width), dt)
    row = pl.BlockSpec((1, slots, width), lambda i: (i, 0, 0))
    return pl.pallas_call(
        fwd_kernel,
        name="forward",
        grid=(batches,),
        out_shape=(
            tok(F32),
            jax.ShapeDtypeStruct((3, batches * slots, width), BF),
            jax.ShapeDtypeStruct((batches, HEADS, slots), F32),
            tok(BF),
            tok(F32),
            tok(F32),
            tok(BF),
            jax.ShapeDtypeStruct((batches, IMGS, width), BF),
        ),
        in_specs=[
            smem_spec(),
            row,
            pl.BlockSpec((1, 1, slots), lambda i: (i, 0, 0)),
            pl.BlockSpec((1, 1, pos.shape[2]), lambda i: (i, 0, 0)),
            pl.BlockSpec((4, width), lambda i: (0, 0)),
            any_spec(),
        ],
        out_specs=(
            row,
            pl.BlockSpec((3, slots, width), lambda i: (0, i, 0)),
            pl.BlockSpec((1, HEADS, slots), lambda i: (i, 0, 0)),
            row,
            row,
            row,
            row,
            pl.BlockSpec((1, IMGS, width), lambda i: (i, 0, 0)),
        ),
        scratch_shapes=[
            pltpu.VMEM((pieces, width, width), BF),
            pltpu.VMEM((slots, slots), F32),
            pltpu.SemaphoreType.DMA((pieces,)),
        ],
        compiler_params=pltpu.CompilerParams(vmem_limit_bytes=VMEM_LIMIT),
    )(role, patch, seg, pos, gain, w)


def norm_back(grad_out, normed, scaled, gain_vec):
    grad_hat = grad_out * gain_vec
    inner = jnp.mean(grad_hat * normed, axis=-1, keepdims=True)
    grad_in = scaled * (grad_hat - jnp.mean(grad_hat, axis=-1, keepdims=True) - normed * inner)
    return grad_in, jnp.sum(grad_out * normed, axis=0, keepdims=True)


def bwd_kernel(
    listed, place, seg, pos, gain, e_in, qkv, lse, x1_in, x2_in, tgt, banks, w_hbm,
    head_out, attn_out, ffn_out, act_out, de_out, mid_out, pred_out, dqkv, du_out, down_out, small,
    w, bias, top_scr, pool_scr, sem,
):
    i = pl.program_id(0)
    role = place[0]
    slots, width = e_in.shape[1:]
    pieces = w_hbm.shape[0]
    cuts = (pieces - 6) // 2

    @pl.when(role == 0)
    def _():
        small[...] = jnp.zeros_like(small)

    @pl.when(role != 0)
    def _():
        order = [2]
        for j in range(cuts):
            order += [6 + cuts + j, 6 + j]
        order += [1, 3, 4, 5]

        @pl.when(i == 0)
        def _():
            for u in order:
                pltpu.make_async_copy(w_hbm.at[u], w.at[u - 1], sem.at[u]).start()
            small[...] = jnp.zeros_like(small)

        def need(u):
            @pl.when(i == 0)
            def _():
                pltpu.make_async_copy(w_hbm.at[u], w.at[u - 1], sem.at[u]).wait()

        seg_row = seg[0]
        seg_col = column_of(seg_row)
        fill_bias(bias, seg_col, seg_row)
        flags = flag_column(pos[0], slots)
        n3, r3 = layer_stats(x2_in[0])
        head_in = (n3 * gain[2:3, :]).astype(BF)
        head_out[0] = head_in
        need(2)
        pred = nn(head_in, w[1])
        valid = jnp.where(seg_col < IMGS, flags, 0).astype(F32)
        diff = pred - tgt[0].astype(F32)
        size = jnp.abs(diff)
        huber = jnp.where(size < 1.0, 0.5 * diff * diff, size - 0.5)
        regress = jnp.sum(jnp.sum(valid * huber, axis=1, keepdims=True), axis=0, keepdims=True)
        count = listed[0] * width
        grad_pred = valid * (jnp.clip(diff, -1.0, 1.0) / count)
        pool_scr[...] = jnp.zeros_like(pool_scr)
        for m in range(IMGS):
            inside = seg_col == m
            tally = jnp.sum(jnp.where(inside, 1.0, 0.0), axis=0, keepdims=True)
            pool_scr[m : m + 1, :] = jnp.sum(jnp.where(inside, pred, 0.0), axis=0, keepdims=True) / tally
        pooled = pool_scr[...]
        length = lax.rsqrt(jnp.sum(pooled * pooled, axis=-1, keepdims=True) + 1e-06)
        unit = pooled * length
        memory = banks[0]
        choices = memory.shape[0]
        logits = nt(unit.astype(BF), memory) / SOFTMAX_TEMPER
        row_id = lax.broadcasted_iota(jnp.int32, logits.shape, 0)
        real = row_id < IMGS
        picked = jnp.where(
            real & (lax.broadcasted_iota(jnp.int32, logits.shape, 1) == place[1] * IMGS + row_id), 1.0, 0.0
        )
        peak = jnp.max(logits, axis=-1, keepdims=True)
        ex = jnp.exp(logits - peak)
        total = jnp.sum(ex, axis=-1, keepdims=True)
        each = peak + jnp.log(total) - jnp.sum(logits * picked, axis=-1, keepdims=True)
        contrast = jnp.sum(jnp.where(real[:, 0:1], each, 0.0), axis=0, keepdims=True)
        scale = choices * MICRO_BATCHES
        grad_logits = (jnp.where(real, ex / total - picked, 0.0) / scale / SOFTMAX_TEMPER).astype(BF)
        grad_unit = nn(grad_logits, memory)
        grad_pool = length * (grad_unit - unit * jnp.sum(grad_unit * unit, axis=1, keepdims=True))
        pool_scr[...] = grad_pool
        for m in range(IMGS):
            inside = seg_col == m
            tally = jnp.sum(jnp.where(inside, 1.0, 0.0), axis=0, keepdims=True)
            grad_pred = grad_pred + jnp.where(inside, pool_scr[m : m + 1, :] / tally, 0.0)
        low = grad_pred.astype(BF)
        pred_out[0] = low
        loss = regress / count + contrast / scale
        small[4:5, :] += jnp.broadcast_to(loss, (1, width))
        grad_top, gain_three = norm_back(nt(low, w[1]), n3, r3, gain[2:3, :])
        small[2:3, :] += gain_three
        top_scr[...] = grad_top
        down = grad_top.astype(BF)
        down_out[0] = down
        n2, r2 = layer_stats(x1_in[0])
        ffn_in = (n2 * gain[1:2, :]).astype(BF)
        ffn_out[0] = ffn_in
        acc = None
        for j in range(cuts):
            need(6 + cuts + j)
            grad_act = nt(down, w[5 + cuts + j])
            need(6 + j)
            hid = nn(ffn_in, w[5 + j])
            th = jnp.tanh(GELU_A * (hid + GELU_B * hid * hid * hid))
            cdf = 0.5 * (1.0 + th)
            act_out[j] = (hid * cdf).astype(BF)
            slope = cdf + hid * (0.5 * (1.0 - th * th)) * (GELU_A * (1.0 + 3.0 * GELU_B * hid * hid))
            du = (grad_act * slope).astype(BF)
            du_out[j] = du
            part = nt(du, w[5 + j])
            acc = part if acc is None else acc + part
        grad_ffn, gain_two = norm_back(acc, n2, r2, gain[1:2, :])
        small[1:2, :] += gain_two
        mid = top_scr[...] + grad_ffn
        top_scr[...] = mid
        mid_low = mid.astype(BF)
        mid_out[0] = mid_low
        need(1)
        de_out[0] = nt(mid_low, w[0]).astype(BF)

        def pair(p, carry):
            cs = pl.ds(pl.multiple_of(p * LANES, LANES), LANES)
            q2, k2, v2, g2 = qkv[0, :, cs], qkv[1, :, cs], qkv[2, :, cs], de_out[0, :, cs]
            k_scaled = k2 * jnp.asarray(HEAD_DIM**-0.5, BF)
            k_t = k2.T
            dq, dk, dv = [], 0.0, 0.0
            for h in range(2):
                s = nt(half(k_scaled, h), q2) + bias[...]
                probs = jnp.exp(s - lse[0, pl.ds(2 * p + h, 1), :])
                dp = nt(half(v2, h), g2)
                centre = jnp.sum(probs * dp, axis=0, keepdims=True)
                ds = (probs * (dp - centre)).astype(BF)
                dv = dv + nn(probs.astype(BF), half(g2, h))
                dk = dk + nn(ds, half(q2, h))
                dq.append(nn(k_t[h * HEAD_DIM : (h + 1) * HEAD_DIM, :], ds))
            dqkv[0, :, cs] = (jnp.concatenate(dq, axis=0) * HEAD_DIM**-0.5).T.astype(BF)
            dqkv[1, :, cs] = (dk * HEAD_DIM**-0.5).astype(BF)
            dqkv[2, :, cs] = dv.astype(BF)
            return carry

        lax.fori_loop(0, HEADS // 2, pair, 0)
        acc = None
        for j in range(3):
            need(3 + j)
            part = nt(dqkv[j], w[2 + j])
            acc = part if acc is None else acc + part
        n1, r1 = layer_stats(e_in[0])
        attn_out[0] = (n1 * gain[0:1, :]).astype(BF)
        grad_attn, gain_one = norm_back(acc, n1, r1, gain[0:1, :])
        small[0:1, :] += gain_one
        start = top_scr[...] + grad_attn
        hidden_slot = flags > 0
        small[3:4, :] += jnp.sum(jnp.where(hidden_slot, start, 0.0), axis=0, keepdims=True)
        de_out[0] = jnp.where(hidden_slot, 0.0, start).astype(BF)


def backward(listed, place, seg, pos, gain, saved, tgt, banks, w):
    e, qkv, lse, x1, x2 = saved
    batches, slots, width = e.shape
    pieces = w.shape[0]
    cuts = (pieces - 6) // 2
    once = pl.Buffered(1)
    tok = lambda n: jax.ShapeDtypeStruct((n, batches * slots, width), BF)
    row_in = pl.BlockSpec((1, slots, width), lambda i: (i, 0, 0), pipeline_mode=once)
    piece = lambda n: pl.BlockSpec((n, slots, width), lambda i: (0, i, 0))
    return pl.pallas_call(
        bwd_kernel,
        name="backward",
        grid=(batches,),
        out_shape=(
            tok(1), tok(1), tok(1), tok(cuts), tok(1), tok(1), tok(1), tok(3), tok(cuts), tok(1),
            jax.ShapeDtypeStruct((SUBLANES, width), F32),
        ),
        in_specs=[
            smem_spec(),
            smem_spec(),
            pl.BlockSpec((1, 1, slots), lambda i: (i, 0, 0)),
            pl.BlockSpec((1, 1, pos.shape[2]), lambda i: (i, 0, 0)),
            pl.BlockSpec((4, width), lambda i: (0, 0)),
            row_in,
            pl.BlockSpec((3, slots, width), lambda i: (0, i, 0), pipeline_mode=once),
            pl.BlockSpec((1, HEADS, slots), lambda i: (i, 0, 0)),
            row_in,
            row_in,
            row_in,
            pl.BlockSpec((1,) + banks.shape[1:], lambda i: (i, 0, 0), pipeline_mode=once),
            any_spec(),
        ],
        out_specs=(
            piece(1), piece(1), piece(1), piece(cuts), piece(1), piece(1), piece(1), piece(3), piece(cuts), piece(1),
            pl.BlockSpec((SUBLANES, width), lambda i: (0, 0)),
        ),
        scratch_shapes=[
            pltpu.VMEM((pieces - 1, width, width), BF),
            pltpu.VMEM((slots, slots), F32),
            pltpu.VMEM((slots, width), F32),
            pltpu.VMEM((SUBLANES, width), F32),
            pltpu.SemaphoreType.DMA((pieces,)),
        ],
        compiler_params=pltpu.CompilerParams(vmem_limit_bytes=VMEM_LIMIT),
    )(listed, place, seg, pos, gain, e, qkv, lse, x1, x2, tgt, banks, w)


def grads_kernel(
    units, plan, cuts, role, owners, patch, mixed, head, attn, ffn, act, de, mid, pred, dqkv, du, down, out,
    rows_scr, x_buf, x_t, g_buf, stage, outbuf, x_sem, g_sem, out_sem,
):
    blocks, rows, width = out.shape
    cols = width // LANES
    lefts = {"patch": patch, "mixed": mixed, "head": head, "attn": attn, "ffn": ffn, "act": act}
    rights = {"de": de, "mid": mid, "pred": pred, "dqkv": dqkv, "du": du, "down": down}

    @pl.when(role[0] == 0)
    def _():
        outbuf[...] = jnp.zeros_like(outbuf)

        def put(b, carry):
            pltpu.make_async_copy(outbuf.at[0], out.at[b], out_sem.at[0]).start()
            return carry

        def done(b, carry):
            pltpu.make_async_copy(outbuf.at[0], out.at[b], out_sem.at[0]).wait()
            return carry

        lax.fori_loop(0, blocks, put, 0)
        lax.fori_loop(0, blocks, done, 0)

    @pl.when(role[0] != 0)
    def _():
        lcopies, rcopies = [], []
        lkeys, rkeys = [], []
        steps = []
        for u, (left, right) in enumerate(plan):
            if not lkeys or lkeys[-1] != left:
                slot = len(lkeys) % 2
                lcopies.append(pltpu.make_async_copy(lefts[left[0]].at[left[1]], x_buf.at[slot], x_sem.at[slot]))
                lkeys.append(left)
                fresh_l = True
            else:
                fresh_l = False
            if not rkeys or rkeys[-1] != right:
                slot = len(rkeys) % 2
                rcopies.append(pltpu.make_async_copy(rights[right[0]].at[right[1]], g_buf.at[slot], g_sem.at[slot]))
                rkeys.append(right)
                fresh_r = True
            else:
                fresh_r = False
            steps.append((u, len(lkeys) - 1, fresh_l, len(rkeys) - 1, fresh_r))
        lcopies[0].start()
        rcopies[0].start()
        for u, li, fresh_l, ri, fresh_r in steps:
            if fresh_l:
                lcopies[li].wait()
                if li + 1 < len(lcopies):
                    lcopies[li + 1].start()
                x_t[...] = x_buf[li % 2].T
            if fresh_r:
                rcopies[ri].wait()
                if ri + 1 < len(rcopies):
                    rcopies[ri + 1].start()
            first, step = units[u]
            wide = 2 * LANES

            def tile(n, carry):
                part = nn(x_t[...], g_buf[ri % 2, :, pl.ds(pl.multiple_of(n * wide, wide), wide)])
                for c in range(2):
                    rows_scr[pl.ds(first * SUBLANES + 2 * n + c, width, stride=step * SUBLANES), :] = part[
                        :, c * LANES : (c + 1) * LANES
                    ]
                return carry

            lax.fori_loop(0, width // wide, tile, 0)

        def block(b, carry):
            slot = lax.rem(b, 2)

            def move(r, carry):
                src = pl.multiple_of(owners[b * rows + r] * SUBLANES, SUBLANES)
                dst = pl.multiple_of(r * SUBLANES, SUBLANES)
                stage[pl.ds(dst, SUBLANES), :] = rows_scr[pl.ds(src, SUBLANES), :]
                return carry

            lax.fori_loop(0, rows, move, 0, unroll=14)

            @pl.when(b >= 2)
            def _():
                pltpu.make_async_copy(outbuf.at[slot], out.at[b - 2], out_sem.at[slot]).wait()

            for c in range(cols):
                outbuf[slot, :, c * LANES : (c + 1) * LANES] = stage[pl.ds(c, rows, stride=SUBLANES), :].astype(BF)
            pltpu.make_async_copy(outbuf.at[slot], out.at[b], out_sem.at[slot]).start()
            return carry

        lax.fori_loop(0, blocks, block, 0)
        for b in (blocks - 2, blocks - 1):
            pltpu.make_async_copy(outbuf.at[b % 2], out.at[b], out_sem.at[b % 2]).wait()


def weight_grads(role, owners, lefts, rights, units, blocks):
    tokens, width = lefts[0].shape[1:]
    cuts = lefts[-1].shape[0]
    total = owners.shape[0]
    rows = total // blocks
    plan = (
        [(("patch", 0), ("de", 0)), (("mixed", 0), ("mid", 0)), (("head", 0), ("pred", 0))]
        + [(("attn", 0), ("dqkv", j)) for j in range(3)]
        + [(("ffn", 0), ("du", j)) for j in range(cuts)]
        + [(("act", j), ("down", 0)) for j in range(cuts)]
    )
    return pl.pallas_call(
        functools.partial(grads_kernel, units, plan, cuts),
        name="weight_grads",
        out_shape=jax.ShapeDtypeStruct((blocks, rows, width), BF),
        in_specs=[smem_spec(), smem_spec()] + [any_spec()] * 12,
        out_specs=any_spec(),
        scratch_shapes=[
            pltpu.VMEM((total * SUBLANES, LANES), F32),
            pltpu.VMEM((2, tokens, width), BF),
            pltpu.VMEM((width, tokens), BF),
            pltpu.VMEM((2, tokens, width), BF),
            pltpu.VMEM((rows * SUBLANES, LANES), F32),
            pltpu.VMEM((2, rows, width), BF),
            pltpu.SemaphoreType.DMA((2,)),
            pltpu.SemaphoreType.DMA((2,)),
            pltpu.SemaphoreType.DMA((2,)),
        ],
        compiler_params=pltpu.CompilerParams(vmem_limit_bytes=VMEM_LIMIT),
    )(role, owners, *lefts, *rights)


def shifted(block, axis, distance):
    devices = range(lax.axis_size(axis))
    route = [(i - distance, i) for i in devices if i - distance in devices]
    return lax.ppermute(block, axis, route)


def adam_update(weight, first_state, second_state, gradient, step_value, decay_rate):
    first_state = BETA_ONE * first_state + (1.0 - BETA_ONE) * gradient
    second_state = BETA_TWO * second_state + (1.0 - BETA_TWO) * gradient * gradient
    fix_one = 1.0 - jnp.power(BETA_ONE, step_value)
    fix_two = 1.0 - jnp.power(BETA_TWO, step_value)
    update = first_state / fix_one / (jnp.sqrt(second_state / fix_two) + ADAM_EPS)
    return (weight - RATE * (update + decay_rate * weight), first_state, second_state)


def body(
    patches,
    segments,
    positions,
    owners,
    master,
    moment_one,
    moment_two,
    teacher,
    gains,
    gain_one,
    gain_two,
    teacher_gains,
    step_count,
):
    core = lax.axis_index("group")
    width = patches.shape[3]
    slots = patches.shape[2]
    row_total = owners.shape[0]
    inner = (row_total - 6 * width) // 2
    units = unit_list(width, inner)
    devices = lax.axis_size("group") * lax.axis_size("dp")
    own_rows = row_total // devices
    role = core.astype(jnp.int32).reshape(1)
    place = jnp.stack([core, lax.axis_index("dp")]).astype(jnp.int32)
    listed = jnp.full((1,), MASKED * lax.axis_size("dp") * MICRO_BATCHES, F32)

    learn = lax.all_gather(master.astype(BF), ("group", "dp"), axis=0)
    teach = lax.all_gather(teacher.astype(BF), ("group", "dp"), axis=0)
    w = place_weights(role, owners, teach, learn, units)
    gain_set = jnp.where(core == 1, gains, teacher_gains)
    patch = patches[:, 0]
    seg = segments
    pos = positions
    e, qkv, lse, mixed, x1, x2, tgt, bank = forward(role, patch, seg, pos, gain_set, w)
    tgt, bank = shifted((tgt, bank), "group", 1)
    banks = lax.all_gather(bank, "dp", axis=1, tiled=True)
    head, attn, ffn, act, de, mid, pred, dqkv, du, down, small = backward(
        listed, place, seg, pos, gain_set, (e, qkv, lse, x1, x2), tgt, banks, w
    )
    flat = lambda a: a.reshape(1, MICRO_BATCHES * slots, width)
    blocked = weight_grads(
        role,
        owners,
        (flat(patch), flat(mixed), head, attn, ffn, act),
        (de, mid, pred, dqkv, du, down),
        units,
        devices,
    )
    owned_grad = lax.psum_scatter(blocked, ("group", "dp"), scatter_dimension=0, tiled=True)
    owned_grad = owned_grad.reshape(own_rows, width).astype(F32)
    square_own = jnp.sum(owned_grad * owned_grad)
    small, square_sum = lax.psum((small, square_own), ("group", "dp"))
    gain_sum, loss_sum = small[0:4], small[4, 0]
    grad_norm = jnp.sqrt(square_sum + jnp.sum(gain_sum * gain_sum))
    factor = jnp.minimum(1.0, CLIP / grad_norm)
    step_value = step_count[0].astype(F32)
    master_new, one_new, two_new = adam_update(
        master, moment_one, moment_two, owned_grad * factor, step_value, DECAY
    )
    gone_new, gtwo_new = adam_update(gains, gain_one, gain_two, gain_sum * factor, step_value, 0.0)[1:]
    teacher_new = EMA_KEEP * teacher + (1.0 - EMA_KEEP) * master_new
    return (
        loss_sum.reshape(1),
        grad_norm.reshape(1),
        one_new,
        two_new,
        master_new,
        teacher_new,
        gone_new,
        gtwo_new,
    )


def solution(mesh):
    rows = P(("group", "dp"), None)
    in_specs = (
        P(None, "dp", None, None),
        P(None, "dp", None),
        P(None, "dp", None),
        P(),
        rows,
        rows,
        rows,
        rows,
        P(),
        P(),
        P(),
        P(),
        P(),
    )
    out_specs = (P(), P(), rows, rows, rows, rows, P(), P())
    return jax.shard_map(body, mesh=mesh, in_specs=in_specs, out_specs=out_specs, check_vma=False)
```

time: 1440 us -> 795 us (0.55)
  waiting for transfers between devices: 898 us -> 535 us
  local copies, waits for them, and re-layouts: 201 us -> 1.27 us
  Pallas kernels: 0 us -> 135 us
  other arithmetic: 92.1 us -> 12.4 us
  matrix products: 69.9 us -> 0 us
  blocking collectives: 120 us -> 79.1 us
  loops' own time: 17.9 us -> 0 us
    reduce_scatter x1, waiting for transfers between devices: 714 us -> 304 us  [body(): lax.psum_scatter(blocked, ('group', 'dp'), scatter_dimension=0, tiled=True)]
    pallas_call x0 -> x4, Pallas kernels: none -> 135 us  [the longest x1 56 us: forward(): pl.pallas_call(fwd_kernel, name='forward', grid=(batches,), out_shape=(to...]
    gather x4 -> x0, local copies, waits for them, and re-layouts: 101 us -> none  [the longest x1 49.4 us: body(): blocked = grad_total[owners].reshape(device_count, own_rows, width)]
    dot_general x16 -> x0, matrix products: 69.9 us -> none  [the longest x10 41.1 us: dense(): return jnp.dot(first_op, second_op, preferred_element_type=jnp.float32)]
    all_gather x2, waiting for transfers between devices: 184 us -> 231 us  [the longest x1 115 us: body(): teach = lax.all_gather(teacher.astype(BF), ('group', 'dp'), axis=0)]
    all_gather x2 -> x1, blocking collectives: 79 us -> 38.9 us  [body(): banks = lax.all_gather(bank, 'dp', axis=1, tiled=True)]
    scatter x1 -> x0, local copies, waits for them, and re-layouts: 39.8 us -> none  [body(): jnp.zeros((row_total,), jnp.int32).at[owners]]
    add x4 -> x0, other arithmetic: 33 us -> none  [the longest x1 33 us: body(): grad_total = grad_total + grad_rows]
  transfers between devices with their start and end apart: 7 -> 5, of which waited for: 3 -> 4; matrix products, arithmetic and copies ran while one was open for 6% -> 1% of each run, Pallas kernels for 0% -> 0%
where the time goes in v1:
time: 795 us; the launch traced here: 784 us
  waiting for transfers between devices  535 us (67%)
  Pallas kernels  135 us (17%)
  blocking collectives  79.1 us (10%)
  between operations  17.7 us (2%)
  other arithmetic  12.4 us (2%)
    reduce_scatter x1, waiting for transfers between devices, body(): lax.psum_scatter(blocked, ('group', 'dp'), scatter_dimension=0, tiled=True)  304 us
    all_gather x1, waiting for transfers between devices, body(): teach = lax.all_gather(teacher.astype(BF), ('group', 'dp'), axis=0)  115 us
    all_gather x1, waiting for transfers between devices, body(): learn = lax.all_gather(master.astype(BF), ('group', 'dp'), axis=0)  115 us
    pallas_call x1, Pallas kernels, forward(): pl.pallas_call(fwd_kernel, name='forward', grid=(batches,), out_shape=(to...  56 us
    pallas_call x1, Pallas kernels, place_weights(): pl.pallas_call(functools.partial(place_kernel, units), name='place_weight...  54.4 us
    psum x1, blocking collectives, body(): small, square_sum = lax.psum((small, square_own), ('group', 'dp'))  40.2 us
    all_gather x1, blocking collectives, body(): banks = lax.all_gather(bank, 'dp', axis=1, tiled=True)  38.9 us
    pallas_call x1, Pallas kernels, backward(): pl.pallas_call(bwd_kernel, name='backward', grid=(batches,), out_shape=(t...  17.2 us
  transfers between devices with their start and end apart: 5, of which 4 were waited for; matrix products, arithmetic and copies ran while one was open for 1% of the time, Pallas kernels for 0%

profile of v1, /device:TPU:0, one launch (start us, length us, event | category | flops | bytes accessed | tf_op | source)
XLA Modules:
  0.0 784.2 jit_solution(15371276167620075286)
XLA Ops:
  7.2 2.1 convert_element_type.14
  9.3 0.0 all-gather.7.cloned.1.call-start
  9.4 2.1 convert_element_type.15
  11.4 0.0 reduce-scatter.2.cloned.1.call-start
  11.5 0.6 broadcast_select_fusion.gain
  12.1 115.5 %all-gather.5.cloned.1.call-done = bf16[10752,768]{1,0:T(8,128)(2,1)} async-done(((bf16[336,768]{1,0:T(8,128)(2,1)}), bf16[10752,768]{1,0:T(8,128)(2,1)}) %all-gather.5.cloned.1.call-update) | async-done | bytes 16515088 | tf_op jit(solution)/shard_map/all_gather | solution.py:653
  127.6 115.1 %all-gather.7.cloned.1.call-done = bf16[10752,768]{1,0:T(8,128)(2,1)} async-done(((bf16[336,768]{1,0:T(8,128)(2,1)}), bf16[10752,768]{1,0:T(8,128)(2,1)}) %all-gather.7.cloned.1.call-update) | async-done | bytes 16515088 | tf_op jit(solution)/shard_map/all_gather | solution.py:652
  242.7 54.4 %place_weights.1.w_hbm = bf16[14,768,768]{2,1,0:T(8,128)(2,1)} custom-call(s32[1]{0:T(128)} %bitcast.role, s32[10752]{0:T(1024)} %owners.3, bf16[32,336,768]{2,1,0:T(8,128)(2,1)} %bitcast.23, bf16[32,336,768]{2,1,0:T(8,128)(2,1)} %bitcast.24), custom_call_target="tpu_custom_call" | custom-call | tf_op jit(solution)/shard_map/place_weights/pallas_call | solution.py:112
  297.1 56.0 %forward.1 = (f32[2,512,768]{2,1,0:T(8,128)}, bf16[3,1024,768]{2,1,0:T(8,128)(2,1)}, f32[2,12,512]{2,1,0:T(8,128)}, bf16[2,512,768]{2,1,0:T(8,128)(2,1)}, f32[2,...) custom-call(s32[1]{0:T(128)} %bitcast.role, ...), custom_call_target="tpu_custom_call" | custom-call | tf_op jit(solution)/shard_map/forward/pallas_call | solution.py:238
  353.0 2.4 collective-permute-start
  355.5 1.3 collective-permute-start.1
  356.7 0.6 pad_add_fusion.place
  357.3 0.4 collective-permute-done.1
  357.8 38.9 %all_gather.19 = bf16[2,64,768]{2,0,1:T(2,128)(2,1)S(1)} all-gather(bf16[2,4,768]{2,0,1:T(2,128)(2,1)S(1)} %copy.21), channel_id=1, replica_groups=mesh['group'=2,'dp'=16] {'dp'}, dimensions={1}, use_global_device_ids=true | all-gather | bytes 208896 | tf_op jit(solution)/shard_map/all_gather | solution.py:661
  396.7 0.7 copy.22.banks
  397.4 17.2 %backward.1 = (bf16[1,1024,768]{2,1,0:T(8,128)(2,1)}, bf16[1,1024,768]{2,1,0:T(8,128)(2,1)}, bf16[1,1024,768]{2,1,0:T(8,128)(2,1)}, bf16[4,1024,768]{2,1,0:T(8,1...) custom-call(f32[1]{0:T(128)} %constant.17.clone.1.listed, ...), custom_call_target="tpu_custom_call" | custom-call | tf_op jit(solution)/shard_map/backward/pallas_call | solution.py:445
  414.6 7.1 weight_grads.1
  422.7 304.2 %reduce-scatter.2.cloned.1.call-done = bf16[1,336,768]{2,1,0:T(8,128)(2,1)} async-done(((bf16[32,336,768]{2,1,0:T(8,128)(2,1)}), bf16[1,336,768]{2,1,0:T(8,128)(2,1)}) %reduce-scatter.2.cloned.1.call-update) | async-done | bytes 516112 | tf_op jit(solution)/shard_map/reduce_scatter | solution.py:674
  727.0 1.9 fusion
  728.9 40.2 %all-reduce = (f32[8,768]{1,0:T(8,128)S(1)}, f32[]{:T(128)}) all-reduce(f32[8,768]{1,0:T(8,128)S(1)} %copy-done.3, f32[]{:T(128)} %fusion), channel_id=1, replica_groups=mesh['group'=2,'dp'=16] {'group','dp'}, use_global_device_ids=true, to_apply=%region_0.1 | all-reduce | flops 6145 | bytes 49160 | tf_op jit(solution)/shard_map/psum | solution.py:677
  769.0 0.6 multiply_reduce_fusion
  769.6 0.5 slice.8
  771.6 0.6 fusion.5
  772.2 4.0 multiply_add_fusion
  (22 shorter events, 0.1 us)
Async XLA Ops:
  7.2 4.3 copy-start.4
  7.2 4.3 copy-start.5
  7.2 120.4 %all-gather.5.cloned.1.call-start = ((), (), s32[]{:S(2)}) async-start(), calls=%async_computation.2 | async-start | bytes 17031168 | tf_op jit(solution)/shard_map/all_gather | solution.py:653
  9.3 233.4 %all-gather.7.cloned.1.call-start = ((), (), s32[]{:S(2)}) async-start(), calls=%async_computation.3 | async-start | bytes 17031168 | tf_op jit(solution)/shard_map/all_gather | solution.py:652
  11.4 715.5 %reduce-scatter.2.cloned.1.call-start = ((), (), s32[]{:S(2)}) async-start(), calls=%async_computation.1 | async-start | bytes 17031168 | tf_op jit(solution)/shard_map/reduce_scatter | solution.py:674
  353.0 44.4 %collective-permute-start = (bf16[2,512,768]{2,1,0:T(8,128)(2,1)}, bf16[2,512,768]{2,1,0:T(8,128)(2,1)}, u32[]{:S(2)}, u32[]{:S(2)}) collective-permute-start(bf16[2,512,768]{2,1,0:T(8,128)(2,1)} %get-tuple-element.32), channel_id=1, source_target_pairs={{0,16},{1,17},{2,18},{3,19},{4,20},{5,21},{6,22},{7,23},{8,24},{9,... | collective-permute-start | bytes 4718600 | tf_op jit(solution)/shard_map/ppermute | solution.py:613
  355.5 2.3 collective-permute-start.1
  421.8 307.1 %copy-start.3 = (f32[8,768]{1,0:T(8,128)S(1)}, f32[8,768]{1,0:T(8,128)}, u32[]{:S(2)}) copy-start(f32[8,768]{1,0:T(8,128)} %get-tuple-element.34) | copy-start | bytes 73732
  421.8 349.8 %copy-start.6 = (f32[4,768]{1,0:T(4,128)S(1)}, f32[4,768]{1,0:T(4,128)}, u32[]{:S(2)}) copy-start(f32[4,768]{1,0:T(4,128)} %param.23) | copy-start | bytes 36868
  421.8 349.8 %copy-start.7 = (f32[4,768]{1,0:T(4,128)S(1)}, f32[4,768]{1,0:T(4,128)}, u32[]{:S(2)}) copy-start(f32[4,768]{1,0:T(4,128)} %param.22) | copy-start | bytes 36868
  421.8 350.4 %copy-start = (f32[336,768]{1,0:T(8,128)S(1)}, f32[336,768]{1,0:T(8,128)}, u32[]{:S(2)}) copy-start(f32[336,768]{1,0:T(8,128)} %param.20) | copy-start | bytes 3096580
  421.8 350.4 %copy-start.1 = (f32[336,768]{1,0:T(8,128)S(1)}, f32[336,768]{1,0:T(8,128)}, u32[]{:S(2)}) copy-start(f32[336,768]{1,0:T(8,128)} %param.17) | copy-start | bytes 3096580
  421.8 350.4 %copy-start.2 = (f32[336,768]{1,0:T(8,128)S(1)}, f32[336,768]{1,0:T(8,128)}, u32[]{:S(2)}) copy-start(f32[336,768]{1,0:T(8,128)} %param.19) | copy-start | bytes 3096580
Sparse Core Ops, SparseCore 0:
  11.5 116.0 all-gather.4
  131.1 111.5 all-gather.6
  422.0 304.9 reduce-scatter.1

commit v2 on v1

--- a/solution.py
+++ b/solution.py
@@ -58,28 +58,486 @@
     return pl.BlockSpec(memory_space=pltpu.SMEM)
 
 
-def place_kernel(units, role, owners, teach, learn, out, rows_scr, inbuf, stage, outbuf, in_sem, out_sem):
-    blocks, rows, width = teach.shape
+MESH = pl.DeviceIdType.MESH
+KERNEL_CHIPS = 16
+
+
+def chip_grid(chips):
+    sizes, turn, left, prime = [1, 1, 1], 0, chips, 2
+    while left > 1:
+        while left % prime:
+            prime += 1
+        sizes[turn % 3] *= prime
+        turn += 1
+        left //= prime
+    return tuple(sizes)
+
+
+def strides_of(grid):
+    return (grid[1] * grid[2], grid[2], 1)
+
+
+def coords_of(index, grid):
+    return (index // (grid[1] * grid[2]), lax.rem(index // grid[2], grid[1]), lax.rem(index, grid[2]))
+
+
+def guarded(conditions, action):
+    conditions = [c for c in conditions if c is not None]
+    if not conditions:
+        return action()
+    both = conditions[0]
+    for c in conditions[1:]:
+        both = jnp.logical_and(both, c)
+    pl.when(both)(action)
+
+
+def lanes_of(width):
+    unit = width // 6
+    orders = [((1, 0, 2), 2), ((2, 0, 1), 2), ((0, 2, 1), 1), ((0, 1, 2), 1)]
+    routes, first = [], 0
+    for order, share in orders:
+        routes.append((order, first, share * unit))
+        first += share * unit
+    return routes
+
+
+def offsets(length):
+    if length <= 2:
+        return list(range(length))
+    return [0] + [sign * far for far in range(1, length) for sign in (1, -1)]
+
+
+def route_events(grid, routes):
+    events = []
+    for c, (order, _, _) in enumerate(routes):
+        stack = [()]
+        for d in order:
+            stack = [r + (o,) for r in stack for o in offsets(grid[d])]
+        events += [(sum(abs(o) * 2**i for i, o in enumerate(r)), c, r) for r in stack]
+    return [(c, r) for _, c, r in sorted(events, key=lambda e: e[0])]
+
+
+def onward(grid, order, r):
+    last = max([i for i in range(3) if r[i]], default=-1)
+    outs = []
+    if last >= 0 and grid[order[last]] > 2:
+        outs.append((order[last], 1 if r[last] > 0 else -1))
+    for d in order[last + 1 :]:
+        if grid[d] == 2:
+            outs.append((d, 1))
+        elif grid[d] > 2:
+            outs += [(d, 1), (d, -1)]
+    return outs
+
+
+def neighbour(me, coords, grid, d, sign):
+    step = strides_of(grid)[d]
+    if grid[d] == 2:
+        return me + (1 - 2 * coords[d]) * step, None
+    place = coords[d] + sign
+    return me + sign * step, jnp.logical_and(place >= 0, place < grid[d])
+
+
+def origin(me, coords, grid, order, r):
+    index, conditions = me, []
+    for d, o in zip(order, r):
+        if o == 0:
+            continue
+        step = strides_of(grid)[d]
+        if grid[d] == 2:
+            index = index + (1 - 2 * coords[d]) * step
+        else:
+            place = coords[d] - o
+            index = index - o * step
+            conditions.append(jnp.logical_and(place >= 0, place < grid[d]))
+    return index, conditions
+
+
+def slot_of(grid, d, sign):
+    first = sum([1 if n <= 2 else 2 for n in grid[:d]])
+    return first if grid[d] <= 2 or sign > 0 else first + 1
+
+
+def slots_of(grid):
+    return sum([1 if n <= 2 else 2 for n in grid])
+
+
+def greet(me, coords, grid, group):
+    barrier = pltpu.get_barrier_semaphore()
+    near = [neighbour(me, coords, grid, d, s) for d in range(3) for s in ((1,) if grid[d] == 2 else (1, -1)) if grid[d] > 1]
+    for index, there in near:
+        guarded([there], lambda: pl.semaphore_signal(barrier, 1, device_id={"dp": index}, device_id_type=MESH))
+    pl.semaphore_signal(barrier, 1, device_id={"group": 1 - group}, device_id_type=MESH)
+    pl.semaphore_wait(barrier, 1 + sum([1 if there is None else there.astype(jnp.int32) for _, there in near]))
+
+
+def gather_kernel(grid, both, out, swap_sem, send_sem, recv_sem):
+    group, me = lax.axis_index("group"), lax.axis_index("dp")
+    coords = coords_of(me, grid)
+    routes = lanes_of(both.shape[2])
+    events = route_events(grid, routes)
+    keep = pltpu.make_async_copy(both.at[group], out.at[me, group], swap_sem.at[2])
+    keep.start()
+    greet(me, coords, grid, group)
+    swap = pltpu.make_async_remote_copy(
+        both.at[1 - group], out.at[me, group], swap_sem.at[0], swap_sem.at[1], {"group": 1 - group}, MESH
+    )
+    swap.start()
+    keep.wait()
+    swap.wait()
+
+    def visit(c, r, act):
+        order, first, wide = routes[c]
+        block, real = origin(me, coords, grid, order, r)
+        part = out.at[block, :, :, first : first + wide]
+
+        def run():
+            copies = []
+            for d, sign in onward(grid, order, r):
+                index, there = neighbour(me, coords, grid, d, sign)
+                copies.append(
+                    (
+                        there,
+                        pltpu.make_async_remote_copy(
+                            part,
+                            part,
+                            send_sem.at[c, slot_of(grid, d, sign), block],
+                            recv_sem.at[c, block],
+                            {"dp": index},
+                            MESH,
+                        ),
+                    )
+                )
+            act(part, recv_sem.at[c, block], any(r), copies)
+
+        guarded(real, run)
+
+    def forward_on(part, arrival_sem, remote, copies):
+        if remote:
+            pltpu.make_async_remote_copy(part, part, swap_sem.at[0], arrival_sem, {"dp": me}, MESH).wait_recv()
+        for there, copy in copies:
+            guarded([there], copy.start)
+
+    def finish(part, arrival_sem, remote, copies):
+        for there, copy in copies:
+            guarded([there], copy.wait_send)
+
+    for c, r in events:
+        visit(c, r, forward_on)
+    for c, r in events:
+        visit(c, r, finish)
+
+
+def gather_weights(both, chips):
+    grid = chip_grid(chips)
+    _, rows, width = both.shape
+    return pl.pallas_call(
+        functools.partial(gather_kernel, grid),
+        name="gather_weights",
+        out_shape=jax.ShapeDtypeStruct((chips, 2, rows, width), BF),
+        in_specs=[pl.BlockSpec(memory_space=pltpu.VMEM)],
+        out_specs=any_spec(),
+        scratch_shapes=[
+            pltpu.SemaphoreType.DMA((3,)),
+            pltpu.SemaphoreType.DMA((4, slots_of(grid), chips)),
+            pltpu.SemaphoreType.DMA((4, chips)),
+        ],
+        compiler_params=pltpu.CompilerParams(
+            collective_id=1, has_side_effects=True, vmem_limit_bytes=VMEM_LIMIT
+        ),
+    )(both)
+
+
+def reduce_kernel(grid, blocked, out, acc, heard, load_sem, half_sem, send_sem, recv_sem):
+    group, me = lax.axis_index("group"), lax.axis_index("dp")
+    coords = coords_of(me, grid)
+    rows, width = out.shape
+    routes = lanes_of(width)
+    events = route_events(grid, routes)[::-1]
+    tall = max([t for t in range(16, 49, 16) if rows % t == 0], default=rows)
+
+    def spot(c, r):
+        return tuple(r[routes[c][0].index(d)] for d in range(3))
+
+    firsts = list(dict.fromkeys([spot(c, r) for c, r in events]))
+    greet(me, coords, grid, group)
+
+    def load(where, act):
+        block, real = origin(me, coords, grid, (0, 1, 2), where)
+        local = pltpu.make_async_copy(blocked.at[1, block], acc.at[block], load_sem.at[block])
+        half = pltpu.make_async_remote_copy(
+            blocked.at[0, block], acc.at[block], half_sem.at[0, block], half_sem.at[1, block], {"group": 1 - group}, MESH
+        )
+        guarded(real, lambda: act(local, half))
+
+    def load_start(local, half):
+        @pl.when(group == 1)
+        def _():
+            half.start()
+            local.start()
+
+    def load_wait(local, half):
+        @pl.when(group == 1)
+        def _():
+            local.wait()
+
+        @pl.when(group == 0)
+        def _():
+            half.wait_recv()
+
+    def load_end(local, half):
+        @pl.when(group == 1)
+        def _():
+            half.wait_send()
+
+    for where in firsts:
+        load(where, load_start)
+
+    def parent(c, r, block):
+        order, first, wide = routes[c]
+        i = max([i for i in range(3) if r[i]])
+        sign = 1 if r[i] > 0 else -1
+        index, _ = neighbour(me, coords, grid, order[i], -sign)
+        slot = slot_of(grid, order[i], sign)
+        return pltpu.make_async_remote_copy(
+            acc.at[block, :, first : first + wide],
+            heard.at[slot, block, :, first : first + wide],
+            send_sem.at[c, block],
+            recv_sem.at[c, slot, block],
+            {"dp": index},
+            MESH,
+        )
+
+    def visit(c, r):
+        order, first, wide = routes[c]
+        block, real = origin(me, coords, grid, order, r)
+
+        def run():
+            children = [(slot_of(grid, d, s), neighbour(me, coords, grid, d, s)[1]) for d, s in onward(grid, order, r)]
+            for slot, there in children:
+                part = heard.at[slot, block, :, first : first + wide]
+                arrival = pltpu.make_async_remote_copy(
+                    part, part, send_sem.at[c, block], recv_sem.at[c, slot, block], {"dp": me}, MESH
+                )
+                guarded([there], arrival.wait_recv)
+
+            if any(r):
+                for slot, there in children:
+
+                    def total(slot=slot):
+                        def piece(k, carry):
+                            at = (pl.ds(pl.multiple_of(k * tall, tall), tall), slice(first, first + wide))
+                            acc[(block,) + at] = (
+                                acc[(block,) + at].astype(F32) + heard[(slot, block) + at].astype(F32)
+                            ).astype(BF)
+                            return carry
+
+                        lax.fori_loop(0, rows // tall, piece, 0)
+
+                    guarded([there], total)
+                parent(c, r, block).start()
+            else:
+
+                def first_piece(k, carry):
+                    at = (pl.ds(pl.multiple_of(k * tall, tall), tall), slice(first, first + wide))
+                    out[at] = acc[(block,) + at].astype(F32)
+                    return carry
+
+                lax.fori_loop(0, rows // tall, first_piece, 0)
+                for slot, there in children:
+
+                    def total(slot=slot):
+                        def piece(k, carry):
+                            at = (pl.ds(pl.multiple_of(k * tall, tall), tall), slice(first, first + wide))
+                            out[at] = out[at] + heard[(slot, block) + at].astype(F32)
+                            return carry
+
+                        lax.fori_loop(0, rows // tall, piece, 0)
+
+                    guarded([there], total)
+
+        guarded(real, run)
+
+    ready = set()
+    for c, r in events:
+        if spot(c, r) not in ready:
+            ready.add(spot(c, r))
+            load(spot(c, r), load_wait)
+        visit(c, r)
+    for c, r in events:
+        if any(r):
+            block, real = origin(me, coords, grid, routes[c][0], r)
+            guarded(real, parent(c, r, block).wait_send)
+    for where in firsts:
+        load(where, load_end)
+
+
+def reduce_grads(blocked, chips):
+    grid = chip_grid(chips)
+    _, _, rows, width = blocked.shape
+    return pl.pallas_call(
+        functools.partial(reduce_kernel, grid),
+        name="reduce_grads",
+        out_shape=jax.ShapeDtypeStruct((rows, width), F32),
+        in_specs=[any_spec()],
+        out_specs=pl.BlockSpec(memory_space=pltpu.VMEM),
+        scratch_shapes=[
+            pltpu.VMEM((chips, rows, width), BF),
+            pltpu.VMEM((slots_of(grid), chips, rows, width), BF),
+            pltpu.SemaphoreType.DMA((chips,)),
+            pltpu.SemaphoreType.DMA((2, chips)),
+            pltpu.SemaphoreType.DMA((4, chips)),
+            pltpu.SemaphoreType.DMA((4, slots_of(grid), chips)),
+        ],
+        compiler_params=pltpu.CompilerParams(
+            collective_id=2, has_side_effects=True, vmem_limit_bytes=VMEM_LIMIT
+        ),
+    )(blocked)
+
+
+def exchange_kernel(tgt, bank, tgt_out, banks, tgt_sem, send_sem, recv_sem):
+    group, me = lax.axis_index("group"), lax.axis_index("dp")
+    chips = banks.shape[0]
+    barrier = pltpu.get_barrier_semaphore()
+
+    def hail(k, carry):
+        pl.semaphore_signal(barrier, 1, device_id=(1 - group, lax.rem(me + k, chips)), device_id_type=MESH)
+        return carry
+
+    lax.fori_loop(0, chips, hail, 0)
+    pl.semaphore_wait(barrier, chips)
+    across = pltpu.make_async_remote_copy(
+        tgt, tgt_out, tgt_sem.at[0], tgt_sem.at[1], {"group": 1 - group}, MESH
+    )
+
+    def note(k):
+        other = lax.rem(me + k, chips)
+        return pltpu.make_async_remote_copy(
+            bank, banks.at[me], send_sem.at[k], recv_sem.at[me], (1 - group, other), MESH
+        )
+
+    @pl.when(group == 0)
+    def _():
+        def give(k, carry):
+            note(k).start()
+            return carry
+
+        def given(k, carry):
+            note(k).wait_send()
+            return carry
+
+        across.start()
+        lax.fori_loop(0, chips, give, 0)
+        lax.fori_loop(0, chips, given, 0)
+        across.wait_send()
+
+    @pl.when(group == 1)
+    def _():
+        def take(k, carry):
+            pltpu.make_async_remote_copy(
+                bank, banks.at[k], send_sem.at[k], recv_sem.at[k], (1 - group, me), MESH
+            ).wait_recv()
+            return carry
+
+        lax.fori_loop(0, chips, take, 0)
+        across.wait_recv()
+
+
+def exchange_targets(tgt, bank, chips):
+    return pl.pallas_call(
+        exchange_kernel,
+        name="exchange_targets",
+        out_shape=(jax.ShapeDtypeStruct(tgt.shape, BF), jax.ShapeDtypeStruct((chips,) + bank.shape, BF)),
+        in_specs=[any_spec(), any_spec()],
+        out_specs=(any_spec(), any_spec()),
+        scratch_shapes=[
+            pltpu.SemaphoreType.DMA((2,)),
+            pltpu.SemaphoreType.DMA((chips,)),
+            pltpu.SemaphoreType.DMA((chips,)),
+        ],
+        compiler_params=pltpu.CompilerParams(collective_id=3, has_side_effects=True),
+    )(tgt, bank)
+
+
+def sum_kernel(grid, tile, out, heard, send_sem, recv_sem):
+    group, me = lax.axis_index("group"), lax.axis_index("dp")
+    coords = coords_of(me, grid)
+    lengths = (2,) + grid
+    mine = (group,) + coords
+    peers = []
+    for s, length in enumerate(lengths):
+        for k in range(1, length):
+            other = lax.rem(mine[s] + k, length)
+            if s == 0:
+                peers.append((s, k, (other, me)))
+            else:
+                peers.append((s, k, (group, me + (other - mine[s]) * strides_of(grid)[s - 1])))
+    barrier = pltpu.get_barrier_semaphore()
+    for _, _, device in peers:
+        pl.semaphore_signal(barrier, 1, device_id=device, device_id_type=MESH)
+    pl.semaphore_wait(barrier, len(peers))
+    out[...] = tile[...]
+    for s, length in enumerate(lengths):
+        if length == 1:
+            continue
+        heard[s, mine[s]] = out[...]
+        copies = [
+            pltpu.make_async_remote_copy(
+                heard.at[s, mine[s]], heard.at[s, mine[s]], send_sem.at[s, k], recv_sem.at[s, mine[s]], device, MESH
+            )
+            for t, k, device in peers
+            if t == s
+        ]
+        for copy in copies:
+            copy.start()
+        for k in range(1, length):
+            other = lax.rem(mine[s] + k, length)
+            pltpu.make_async_remote_copy(
+                heard.at[s, other], heard.at[s, other], send_sem.at[s, k], recv_sem.at[s, other], (group, me), MESH
+            ).wait_recv()
+        total = heard[s, 0]
+        for k in range(1, length):
+            total = total + heard[s, k]
+        out[...] = total
+        for copy in copies:
+            copy.wait_send()
+
+
+def sum_tiles(tile, chips):
+    grid = chip_grid(chips)
+    most = max((2,) + grid)
+    return pl.pallas_call(
+        functools.partial(sum_kernel, grid),
+        name="sum_tiles",
+        out_shape=jax.ShapeDtypeStruct(tile.shape, F32),
+        in_specs=[pl.BlockSpec(memory_space=pltpu.VMEM)],
+        out_specs=pl.BlockSpec(memory_space=pltpu.VMEM),
+        scratch_shapes=[
+            pltpu.VMEM((4, most) + tile.shape, F32),
+            pltpu.SemaphoreType.DMA((4, most)),
+            pltpu.SemaphoreType.DMA((4, most)),
+        ],
+        compiler_params=pltpu.CompilerParams(collective_id=4, has_side_effects=True),
+    )(tile)
+
+
+def place_kernel(units, owners, model, out, rows_scr, inbuf, stage, outbuf, in_sem, out_sem):
+    chips, cores, rows, width = model.shape
+    blocks = cores * chips
     cols = width // LANES
 
     def fetch(b, slot):
-        @pl.when(role[0] == 0)
-        def _():
-            pltpu.make_async_copy(teach.at[b], inbuf.at[slot], in_sem.at[slot]).start()
-
-        @pl.when(role[0] != 0)
-        def _():
-            pltpu.make_async_copy(learn.at[b], inbuf.at[slot], in_sem.at[slot]).start()
-
-    fetch(0, 0)
+        return pltpu.make_async_copy(model.at[lax.rem(b, chips), b // chips], inbuf.at[slot], in_sem.at[slot])
+
+    fetch(0, 0).start()
 
     def block(b, carry):
         slot = lax.rem(b, 2)
-        pltpu.make_async_copy(teach.at[b], inbuf.at[slot], in_sem.at[slot]).wait()
+        fetch(b, slot).wait()
 
         @pl.when(b + 1 < blocks)
         def _():
-            fetch(b + 1, 1 - slot)
+            fetch(b + 1, 1 - slot).start()
 
         for c in range(cols):
             stage[pl.ds(c, rows, stride=SUBLANES), :] = inbuf[slot, :, c * LANES : (c + 1) * LANES].astype(F32)
@@ -106,14 +564,14 @@
         pltpu.make_async_copy(outbuf.at[u % 2], out.at[u], out_sem.at[u % 2]).wait()
 
 
-def place_weights(role, owners, teach, learn, units):
-    blocks, rows, width = teach.shape
+def place_weights(owners, model, units):
+    _, _, rows, width = model.shape
     total = owners.shape[0]
     return pl.pallas_call(
         functools.partial(place_kernel, units),
         name="place_weights",
         out_shape=jax.ShapeDtypeStruct((len(units), width, width), BF),
-        in_specs=[smem_spec(), smem_spec(), any_spec(), any_spec()],
+        in_specs=[smem_spec(), any_spec()],
         out_specs=any_spec(),
         scratch_shapes=[
             pltpu.VMEM((total * SUBLANES, LANES), F32),
@@ -124,7 +582,7 @@
             pltpu.SemaphoreType.DMA((2,)),
         ],
         compiler_params=pltpu.CompilerParams(vmem_limit_bytes=VMEM_LIMIT),
-    )(role, owners, teach, learn)
+    )(owners, model)
 
 
 def layer_stats(tensor):
@@ -607,12 +1065,6 @@
     )(role, owners, *lefts, *rights)
 
 
-def shifted(block, axis, distance):
-    devices = range(lax.axis_size(axis))
-    route = [(i - distance, i) for i in devices if i - distance in devices]
-    return lax.ppermute(block, axis, route)
-
-
 def adam_update(weight, first_state, second_state, gradient, step_value, decay_rate):
     first_state = BETA_ONE * first_state + (1.0 - BETA_ONE) * gradient
     second_state = BETA_TWO * second_state + (1.0 - BETA_TWO) * gradient * gradient
@@ -643,22 +1095,27 @@
     row_total = owners.shape[0]
     inner = (row_total - 6 * width) // 2
     units = unit_list(width, inner)
-    devices = lax.axis_size("group") * lax.axis_size("dp")
+    chips = lax.axis_size("dp")
+    devices = lax.axis_size("group") * chips
     own_rows = row_total // devices
     role = core.astype(jnp.int32).reshape(1)
     place = jnp.stack([core, lax.axis_index("dp")]).astype(jnp.int32)
     listed = jnp.full((1,), MASKED * lax.axis_size("dp") * MICRO_BATCHES, F32)
 
-    learn = lax.all_gather(master.astype(BF), ("group", "dp"), axis=0)
-    teach = lax.all_gather(teacher.astype(BF), ("group", "dp"), axis=0)
-    w = place_weights(role, owners, teach, learn, units)
+    both = jnp.stack([teacher, master]).astype(BF)
+    if chips <= KERNEL_CHIPS:
+        model = gather_weights(both, chips)
+    else:
+        parts = lax.all_gather(both, ("dp", "group"), axis=1)
+        model = jnp.where(core == 1, parts[1], parts[0]).reshape(chips, 2, own_rows, width)
+    w = place_weights(owners, model, units)
     gain_set = jnp.where(core == 1, gains, teacher_gains)
     patch = patches[:, 0]
     seg = segments
     pos = positions
     e, qkv, lse, mixed, x1, x2, tgt, bank = forward(role, patch, seg, pos, gain_set, w)
-    tgt, bank = shifted((tgt, bank), "group", 1)
-    banks = lax.all_gather(bank, "dp", axis=1, tiled=True)
+    tgt, banks = exchange_targets(tgt, bank, chips)
+    banks = jnp.swapaxes(banks, 0, 1).reshape(MICRO_BATCHES, chips * IMGS, width)
     head, attn, ffn, act, de, mid, pred, dqkv, du, down, small = backward(
         listed, place, seg, pos, gain_set, (e, qkv, lse, x1, x2), tgt, banks, w
     )
@@ -671,11 +1128,15 @@
         units,
         devices,
     )
-    owned_grad = lax.psum_scatter(blocked, ("group", "dp"), scatter_dimension=0, tiled=True)
-    owned_grad = owned_grad.reshape(own_rows, width).astype(F32)
+    if chips <= KERNEL_CHIPS:
+        owned_grad = reduce_grads(blocked.reshape(2, chips, own_rows, width), chips)
+    else:
+        owned_grad = lax.psum_scatter(blocked, ("group", "dp"), scatter_dimension=0, tiled=True)
+        owned_grad = owned_grad.reshape(own_rows, width).astype(F32)
     square_own = jnp.sum(owned_grad * owned_grad)
-    small, square_sum = lax.psum((small, square_own), ("group", "dp"))
-    gain_sum, loss_sum = small[0:4], small[4, 0]
+    row_id = lax.broadcasted_iota(jnp.int32, small.shape, 0)
+    small = sum_tiles(jnp.where(row_id == 5, square_own, small), chips)
+    gain_sum, loss_sum, square_sum = small[0:4], small[4, 0], small[5, 0]
     grad_norm = jnp.sqrt(square_sum + jnp.sum(gain_sum * gain_sum))
     factor = jnp.minimum(1.0, CLIP / grad_norm)
     step_value = step_count[0].astype(F32)

time: 795 us -> 512 us (0.64)
  waiting for transfers between devices: 535 us -> 0 us
  Pallas kernels: 135 us -> 484 us
  blocking collectives: 79.1 us -> 0 us
  between operations: 17.7 us -> 4.47 us
    pallas_call x0 -> x4, Pallas kernels: none -> 350 us  [the longest x1 196 us: reduce_grads(): pl.pallas_call(functools.partial(reduce_kernel, grid), name='reduce_grads...]
    reduce_scatter x1 -> x0, waiting for transfers between devices: 304 us -> none  [body(): lax.psum_scatter(blocked, ('group', 'dp'), scatter_dimension=0, tiled=True)]
    all_gather x2 -> x0, waiting for transfers between devices: 231 us -> none  [the longest x1 115 us: body(): teach = lax.all_gather(teacher.astype(BF), ('group', 'dp'), axis=0)]
    psum x1 -> x0, blocking collectives: 40.2 us -> none  [body(): small, square_sum = lax.psum((small, square_own), ('group', 'dp'))]
    all_gather x1 -> x0, blocking collectives: 38.9 us -> none  [body(): banks = lax.all_gather(bank, 'dp', axis=1, tiled=True)]
  transfers between devices with their start and end apart: 5 -> 0, of which waited for: 4 -> 0; matrix products, arithmetic and copies ran while one was open for 1% -> 0% of each run, Pallas kernels for 0% -> 0%
where the time goes in v2:
time: 512 us; the launch traced here: 507 us
  Pallas kernels  484 us (95%)
  other arithmetic  14.8 us (3%)
    pallas_call x1, Pallas kernels, reduce_grads(): pl.pallas_call(functools.partial(reduce_kernel, grid), name='reduce_grads...  196 us
    pallas_call x1, Pallas kernels, gather_weights(): pl.pallas_call(functools.partial(gather_kernel, grid), name='gather_weigh...  133 us
    pallas_call x1, Pallas kernels, forward(): pl.pallas_call(fwd_kernel, name='forward', grid=(batches,), out_shape=(to...  55.4 us
    pallas_call x1, Pallas kernels, place_weights(): pl.pallas_call(functools.partial(place_kernel, units), name='place_weight...  54.7 us
    pallas_call x1, Pallas kernels, backward(): pl.pallas_call(bwd_kernel, name='backward', grid=(batches,), out_shape=(t...  17.2 us
    pallas_call x1, Pallas kernels, sum_tiles(): pl.pallas_call(functools.partial(sum_kernel, grid), name='sum_tiles', out...  17.1 us

profile of v2, /device:TPU:0, one launch (start us, length us, event | category | flops | bytes accessed | tf_op | source)
XLA Modules:
  0.0 506.7 jit_solution(5530860617355461314)
XLA Ops:
  0.6 1.6 convert_bitcast_fusion
  2.3 1.1 pad_maximum_fusion.both
  3.3 132.6 %gather_weights.1.model = bf16[16,2,336,768]{3,2,1,0:T(8,128)(2,1)} custom-call(bf16[2,336,768]{2,1,0:T(8,128)(2,1)} %pad_maximum_fusion.both), custom_call_target="tpu_custom_call" | custom-call | tf_op jit(solution)/shard_map/gather_weights/pallas_call | solution.py:234
  135.9 0.0 copy-start.2
  135.9 0.0 copy-start.3
  135.9 54.7 %place_weights.1.w_hbm = bf16[14,768,768]{2,1,0:T(8,128)(2,1)} custom-call(s32[10752]{0:T(1024)} %owners.3, bf16[16,2,336,768]{3,2,1,0:T(8,128)(2,1)} %gather_weights.1.model), custom_call_target="tpu_custom_call" | custom-call | tf_op jit(solution)/shard_map/place_weights/pallas_call | solution.py:570
  190.7 0.6 broadcast_select_fusion.1.gain
  191.3 55.4 %forward.1 = (f32[2,512,768]{2,1,0:T(8,128)}, bf16[3,1024,768]{2,1,0:T(8,128)(2,1)}, f32[2,12,512]{2,1,0:T(8,128)}, bf16[2,512,768]{2,1,0:T(8,128)(2,1)}, f32[2,...) custom-call(s32[1]{0:T(128)} %bitcast.role, ...), custom_call_target="tpu_custom_call" | custom-call | tf_op jit(solution)/shard_map/forward/pallas_call | solution.py:696
  246.7 4.0 exchange_targets.1
  250.7 1.0 copy.21
  251.7 0.7 reshape.42.banks
  252.5 0.6 pad_add_fusion.place
  253.1 17.2 %backward.1 = (bf16[1,1024,768]{2,1,0:T(8,128)(2,1)}, bf16[1,1024,768]{2,1,0:T(8,128)(2,1)}, bf16[1,1024,768]{2,1,0:T(8,128)(2,1)}, bf16[4,1024,768]{2,1,0:T(8,1...) custom-call(f32[1]{0:T(128)} %constant.8.clone.1.listed, ...), custom_call_target="tpu_custom_call" | custom-call | tf_op jit(solution)/shard_map/backward/pallas_call | solution.py:903
  270.2 7.1 %weight_grads.1 = bf16[32,336,768]{2,1,0:T(8,128)(2,1)} custom-call(s32[1]{0:T(128)} %bitcast.role, s32[10752]{0:T(1024)} %owners.3, bf16[1,1024,768]{2,1,0:T(8,128)(2,1)} %bitcast.18, bf16[1,1024,768]{2,1,0:T(8,128)(2,1)} %bitcast.19, bf16[1,1024,768]{2,1,0:T(8,128)(2,1)} %get-tuple-element.39.head, bf16[1,1024,768]{2,1,0:T(8,128)(2,1)} %get-tuple-element.40.attn, ...), custom_call_target="tpu_custom_call" | custom-call | tf_op jit(solution)/shard_map/weight_grads/pallas_call | solution.py:1047
  277.4 0.0 copy-start.1
  277.4 0.0 copy-start.4
  277.4 196.2 %reduce_grads.1 = f32[336,768]{1,0:T(8,128)} custom-call(bf16[2,16,336,768]{3,2,1,0:T(8,128)(2,1)} %bitcast.16), custom_call_target="tpu_custom_call" | custom-call | tf_op jit(solution)/shard_map/reduce_grads/pallas_call | solution.py:378
  473.7 2.2 multiply_reduce_fusion
  475.8 1.3 broadcast_select_fusion.tile
  477.2 17.1 %sum_tiles.1 = f32[8,768]{1,0:T(8,128)} custom-call(f32[8,768]{1,0:T(8,128)} %broadcast_select_fusion.tile), custom_call_target="tpu_custom_call" | custom-call | tf_op jit(solution)/shard_map/sum_tiles/pallas_call | solution.py:509
  494.3 1.3 fusion.3
  495.6 1.3 multiply_reduce_fusion.1
  498.3 1.4 fusion.1
  500.4 4.7 multiply_add_fusion
  (7 shorter events, 0.0 us)
Async XLA Ops:
  135.9 54.8 %copy-start.2 = (f32[4,768]{1,0:T(4,128)S(1)}, f32[4,768]{1,0:T(4,128)}, u32[]{:S(2)}) copy-start(f32[4,768]{1,0:T(4,128)} %param.21) | copy-start | bytes 36868
  135.9 54.8 %copy-start.3 = (f32[4,768]{1,0:T(4,128)S(1)}, f32[4,768]{1,0:T(4,128)}, u32[]{:S(2)}) copy-start(f32[4,768]{1,0:T(4,128)} %param.24) | copy-start | bytes 36868
  277.4 198.4 %copy-start.1 = (f32[8,768]{1,0:T(8,128)S(1)}, f32[8,768]{1,0:T(8,128)}, u32[]{:S(2)}) copy-start(f32[8,768]{1,0:T(8,128)} %get-tuple-element.49) | copy-start | bytes 73732
  277.4 220.9 %copy-start.4 = (f32[4,768]{1,0:T(4,128)S(1)}, f32[4,768]{1,0:T(4,128)}, u32[]{:S(2)}) copy-start(f32[4,768]{1,0:T(4,128)} %param.23) | copy-start | bytes 36868
  473.6 26.8 %copy-start = (f32[336,768]{1,0:T(8,128)S(1)}, f32[336,768]{1,0:T(8,128)}, u32[]{:S(2)}) copy-start(f32[336,768]{1,0:T(8,128)} %reduce_grads.1) | copy-start | bytes 3096580
